TPU v7x, 256 devices: a whole 4x4x8 slice. The times are simulated.
256 devices in a mesh: lat: 4 (over z_lo, core), lon: 16 (over z_hi, y), tm: 4 (over x).
Axes of the slice: x: 4, y: 4, z: 8 (z_hi: 4, z_lo: 2; z = z_hi * 2 + z_lo), core: 2. Of those that a mesh axis runs over, the one named last changes fastest.
Arguments:
- signal: bfloat16 [4, 78, 32, 2048], P('tm', None, 'lat', 'lon'), may hold values from -6 to 6
- dictionary: bfloat16 [64, 9984], P('lon'), may hold values from -0.0625 to 0.0625
- codes_init: float32 [4, 64, 8, 512], P('tm', None, 'lat', 'lon'), may hold values from -3 to 3
- thresholds: float32 [64], replicated, may hold values from 0.2 to 2
Outputs:
- codes: float32 [4, 64, 8, 512], P('tm', None, 'lat', 'lon')
- dict_grad: float32 [64, 9984], P('lon')
All inputs are finite; a program needn't handle non-finite values.
Results may differ from a plain program's by a relative error of at most 0.0044.
Values may be sent and summed in bfloat16 or wider, within the bound.
No kernel may reach another device: no remote copies, remote signals or barrier semaphores. Data moves between devices by JAX's collectives and lax.ppermute only.
A program may use at most 128 MiB of HBM per device.

v0:
```python
import math

import jax
import jax.numpy as jnp
from jax import lax
from jax.sharding import PartitionSpec as P

ITERS = 2


STEP_SIZE = 0.5


def passed_along(shard, axis, by):
    peers = lax.axis_size(axis)
    pairs = [(i, i + by) for i in range(peers) if 0 <= i + by < peers]
    return lax.ppermute(shard, axis, pairs)


def shifted(block, axis, distance):
    devices = range(lax.axis_size(axis))
    route = [((i - distance) % len(devices), i) for i in devices]
    return lax.ppermute(block, axis, route)


def combos():
    return [(delay, down, right) for delay in (0, 1) for down in (0, 1) for right in (0, 1)]


def to_atoms(local, channels, count):
    shaped = local.reshape(channels, 4, 4, 2, 2, 2, count)
    return shaped.transpose(6, 3, 0, 4, 1, 5, 2).reshape(count, 2 * channels * 64)


def extend_codes(coded):
    atoms, rows, columns = coded.shape
    earlier = passed_along(coded, "tm", 1)
    both = jnp.stack([coded, earlier])
    above = passed_along(both[:, :, -1:, :], "lat", 1)
    both = jnp.concatenate([above, both], axis=2)
    beside = shifted(both[:, :, :, -1:], "lon", 1)
    both = jnp.concatenate([beside, both], axis=3)
    pieces = [
        both[delay, :, 1 - down : 1 - down + rows, 1 - right : 1 - right + columns]
        for delay, down, right in combos()
    ]
    return jnp.stack(pieces).reshape(8 * atoms, rows * columns)


def body(signal, dictionary, codes_init, thresholds):
    channels = signal.shape[1]
    rows = signal.shape[2] // 4
    columns = signal.shape[3] // 4
    patch = channels * 16
    gathered = lax.all_gather(dictionary, "lon", axis=0, tiled=True)
    atoms = gathered.shape[0]
    blocks = (
        gathered.reshape(atoms, 2, channels, 2, 4, 2, 4)
        .transpose(1, 3, 5, 2, 4, 6, 0)
        .reshape(8, patch, atoms)
    )
    synth_matrix = blocks.transpose(1, 0, 2).reshape(patch, 8 * atoms)
    target = (
        signal[0]
        .reshape(channels, rows, 4, columns, 4)
        .transpose(0, 2, 4, 1, 3)
        .reshape(patch, rows * columns)
    )

    def residual_of(current):
        stacked = extend_codes(current.astype(jnp.bfloat16).reshape(atoms, rows, columns))
        synth = jnp.dot(synth_matrix, stacked, preferred_element_type=jnp.float32)
        return ((synth - target).astype(jnp.bfloat16), stacked)

    adjoint_matrix = blocks.transpose(2, 0, 1).reshape(atoms, 8 * patch)
    current = codes_init[0].reshape(atoms, rows * columns)
    moving = current
    momentum_now = 1.0
    shrink = STEP_SIZE * thresholds[:, None]
    for turn in range(ITERS):
        residual, stacked = residual_of(moving)
        frame = residual.reshape(patch, rows, columns)
        later = passed_along(frame, "tm", -1)
        both = jnp.stack([frame, later])
        below = passed_along(both[:, :, :1, :], "lat", -1)
        both = jnp.concatenate([both, below], axis=2)
        beside = shifted(both[:, :, :, :1], "lon", -1)
        both = jnp.concatenate([both, beside], axis=3)
        pieces = [
            both[delay, :, down : down + rows, right : right + columns]
            for delay, down, right in combos()
        ]
        adjoint_stacked = jnp.stack(pieces).reshape(8 * patch, rows * columns)
        descent = moving - STEP_SIZE * jnp.dot(
            adjoint_matrix, adjoint_stacked, preferred_element_type=jnp.float32
        )
        updated = jnp.sign(descent) * jnp.maximum(jnp.abs(descent) - shrink, 0.0)
        momentum_next = (1.0 + math.sqrt(1.0 + 4.0 * momentum_now * momentum_now)) / 2.0
        moving = updated + (momentum_now - 1.0) / momentum_next * (updated - current)
        current = updated
        momentum_now = momentum_next
    residual, stacked = residual_of(current)
    positions = lax.axis_size("tm") * lax.axis_size("lat") * lax.axis_size("lon") * rows * columns
    scale = 1.0 / math.sqrt(positions)
    owned_rows = atoms // lax.axis_size("lon")
    local = lax.dot_general(
        residual, stacked, (((1,), (1,)), ((), ())), preferred_element_type=jnp.float32
    )
    total = lax.psum(to_atoms(local, channels, atoms) * scale, ("lat", "lon", "tm"))
    mine = lax.dynamic_slice_in_dim(total, lax.axis_index("lon") * owned_rows, owned_rows, 0)
    return (current.reshape(1, atoms, rows, columns), mine)


def solution(mesh):
    placed = (P("tm", None, "lat", "lon"), P("lon", None), P("tm", None, "lat", "lon"), P())
    return jax.shard_map(
        body,
        mesh=mesh,
        in_specs=placed,
        out_specs=(P("tm", None, "lat", "lon"), P("lon", None)),
        check_vma=False,
    )
```

profile of v0, /device:TPU:1, one launch (start us, length us, event | category | flops | bytes accessed | tf_op | source)
XLA Modules:
  0.0 631.8 jit_solution(5299699721707933311)
XLA Ops:
  8.7 3.9 collective-permute-start
  13.5 4.9 collective-permute-start.1
  24.1 3.8 collective-permute-done.2
  28.3 38.2 %all-gather.3.cloned.1.call-done = bf16[16,4,9984]{2,1,0:T(4,128)(2,1)} async-done(((bf16[1,4,9984]{2,1,0:T(4,128)(2,1)}), bf16[16,4,9984]{2,1,0:T(4,128)(2,1)}) %all-gather.3.cloned.1.call-update) | async-done | bytes 1277968 | tf_op jit(solution)/shard_map/all_gather | solution.py:55
  66.6 89.3 %reshape.84 = bf16[64,2,78,2,4,2,4]{6,5,4,3,2,1,0:T(2,128)(2,1)} reshape(bf16[16,4,9984]{2,1,0:T(4,128)(2,1)} %all-gather.3.cloned.1.call-done) | data formatting | bytes 2555904 | tf_op jit(solution)/shard_map/reshape | solution.py:58
  155.9 86.1 %copy.69 = bf16[64,2,78,2,4,2,4]{0,6,4,2,5,3,1:T(4,128)(2,1)S(1)} copy(bf16[64,2,78,2,4,2,4]{6,5,4,3,2,1,0:T(2,128)(2,1)} %reshape.84) | data formatting | bytes 2555904 | tf_op jit(solution)/shard_map/transpose | solution.py:59
  241.9 2.8 copy.51
  244.7 1.7 fusion.3
  247.7 4.8 collective-permute-done.3
  252.5 5.5 collective-permute-start.4
  258.0 2.9 collective-permute-done.4
  260.9 3.8 collective-permute-start.5
  266.1 1.8 copy.55
  267.9 3.5 reshape.68
  271.4 1.9 fusion.15
  273.3 3.1 collective-permute-start.6
  277.3 3.4 collective-permute-start.7
  281.7 7.3 %collective-permute-done.8 = bf16[2,64,3,1]{1,3,2,0:T(2,128)(2,1)S(1)} collective-permute-done((bf16[2,64,3,1]{1,3,2,0:T(2,128)(2,1)S(1)}, bf16[2,64,3,1]{1,3,2,0:T(2,128)(2,1)S(1)}, u32[]{:S(2)}, u32[]{:S(2)}) %collective-permute-start.8) | collective-permute-done | bytes 800 | tf_op jit(solution)/shard_map/ppermute | solution.py:23
  292.3 6.7 %collective-permute-done.9 = bf16[1248,2,32]{0,2,1:T(8,128)(2,1)S(1)} collective-permute-done((bf16[1248,2,32]{0,2,1:T(8,128)(2,1)S(1)}, bf16[1248,2,32]{0,2,1:T(8,128)(2,1)S(1)}, u32[]{:S(2)}, u32[]{:S(2)}) %collective-permute-start.9) | collective-permute-done | bytes 159776 | tf_op jit(solution)/shard_map/ppermute | solution.py:17
  299.1 2.2 collective-permute-start.10
  301.3 5.6 collective-permute-done.10
  310.3 1.8 copy.58
  312.1 3.5 reshape.73
  315.6 2.5 fusion.16
  318.1 3.6 collective-permute-start.12
  322.6 3.7 collective-permute-start.13
  327.3 6.7 %collective-permute-done.14 = bf16[2,64,3,1]{1,3,2,0:T(2,128)(2,1)S(1)} collective-permute-done((bf16[2,64,3,1]{1,3,2,0:T(2,128)(2,1)S(1)}, bf16[2,64,3,1]{1,3,2,0:T(2,128)(2,1)S(1)}, u32[]{:S(2)}, u32[]{:S(2)}) %collective-permute-start.14) | collective-permute-done | bytes 800 | tf_op jit(solution)/shard_map/ppermute | solution.py:23
  336.3 2.7 multiply_bitcast_fusion
  339.0 7.9 %copy.64 = f32[64,2,78,2,4,2,4]{0,6,5,4,3,2,1:T(4,128)} copy(f32[64,2,78,2,4,2,4]{2,0,5,3,1,6,4:T(8,128)} %multiply_bitcast_fusion) | data formatting | bytes 5111808 | tf_op jit(solution)/shard_map/mul | solution.py:109
  347.0 269.4 %all-reduce.2.cloned.1.call-done = f32[64,9984]{0,1:T(8,128)} async-done(((f32[64,9984]{0,1:T(8,128)}), f32[64,9984]{0,1:T(8,128)}) %all-reduce.2.cloned.1.call-update) | async-done | bytes 2555920 | tf_op jit(solution)/shard_map/psum | solution.py:109
  616.4 4.7 constant_dynamic-slice_fusion
  621.1 3.9 copy.65
  (91 shorter events, 23.5 us)
Async XLA Ops:
  7.2 59.4 %all-gather.3.cloned.1.call-start = ((), (), s32[]{:S(2)}) async-start(), calls=%async_computation.1 | async-start | bytes 1357824 | tf_op jit(solution)/shard_map/all_gather | solution.py:55
  7.9 608.5 %all-reduce.2.cloned.1.call-start = ((), (), s32[]{:S(2)}) async-start(), calls=%async_computation | async-start | bytes 10223616 | tf_op jit(solution)/shard_map/psum | solution.py:109
  8.7 4.8 collective-permute-start
  13.5 5.8 collective-permute-start.1
  19.3 8.6 %collective-permute-start.2 = (bf16[2,64,3,1]{1,3,2,0:T(2,128)(2,1)S(1)}, bf16[2,64,3,1]{1,3,2,0:T(2,128)(2,1)S(1)}, u32[]{:S(2)}, u32[]{:S(2)}) collective-permute-start(bf16[2,64,3,1]{1,3,2,0:T(2,128)(2,1)S(1)} %pad_maximum_fusion.21), channel_id=1, source_target_pairs={{60,0},{0,4},{4,8},{8,12},{12,16},{16,20},{20,24},{24,28},{28,32},... | collective-permute-start | bytes 2312 | tf_op jit(solution)/shard_map/ppermute | solution.py:23
  244.7 13.2 %copy-start.1 = (f32[64]{0:T(128)S(1)}, f32[64]{0:T(128)}, u32[]{:S(2)}) copy-start(f32[64]{0:T(128)} %param.7) | copy-start | bytes 772
  246.4 6.1 collective-permute-start.3
  252.5 8.4 %collective-permute-start.4 = (bf16[2,1248,1,32]{1,3,2,0:T(8,128)(2,1)S(1)}, bf16[2,1248,1,32]{1,3,2,0:T(8,128)(2,1)S(1)}, u32[]{:S(2)}, u32[]{:S(2)}) collective-permute-start(bf16[2,1248,1,32]{1,3,2,0:T(8,128)(2,1)S(1)} %pad_maximum_fusion.7), channel_id=1, source_target_pairs={{64,0},{128,64},{192,128},{65,1},{129,65},{193,129},{66,2},{130,66... | collective-permute-start | bytes 479240 | tf_op jit(solution)/shard_map/ppermute | solution.py:17
  260.9 4.8 collective-permute-start.5
  267.9 3.5 copy-start
  273.3 3.9 collective-permute-start.6
  277.3 4.3 collective-permute-start.7
  281.6 7.4 %collective-permute-start.8 = (bf16[2,64,3,1]{1,3,2,0:T(2,128)(2,1)S(1)}, bf16[2,64,3,1]{1,3,2,0:T(2,128)(2,1)S(1)}, u32[]{:S(2)}, u32[]{:S(2)}) collective-permute-start(bf16[2,64,3,1]{1,3,2,0:T(2,128)(2,1)S(1)} %pad_maximum_fusion.20), channel_id=1, source_target_pairs={{60,0},{0,4},{4,8},{8,12},{12,16},{16,20},{20,24},{24,28},{28,32},... | collective-permute-start | bytes 2312 | tf_op jit(solution)/shard_map/ppermute | solution.py:23
  291.0 8.0 %collective-permute-start.9 = (bf16[1248,2,32]{0,2,1:T(8,128)(2,1)S(1)}, bf16[1248,2,32]{0,2,1:T(8,128)(2,1)S(1)}, u32[]{:S(2)}, u32[]{:S(2)}) collective-permute-start(bf16[1248,2,32]{0,2,1:T(8,128)(2,1)S(1)} %bitcast.127), channel_id=1, source_target_pairs={{1,0},{2,1},{3,2},{5,4},{6,5},{7,6},{9,8},{10,9},{11,10},{13,12},{... | collective-permute-start | bytes 479240 | tf_op jit(solution)/shard_map/ppermute | solution.py:17
  299.1 7.9 %collective-permute-start.10 = (bf16[2,1248,1,32]{1,3,2,0:T(8,128)(2,1)S(1)}, bf16[2,1248,1,32]{1,3,2,0:T(8,128)(2,1)S(1)}, u32[]{:S(2)}, u32[]{:S(2)}) collective-permute-start(bf16[2,1248,1,32]{1,3,2,0:T(8,128)(2,1)S(1)} %pad_maximum_fusion.4), channel_id=1, source_target_pairs={{64,0},{128,64},{192,128},{65,1},{129,65},{193,129},{66,2},{130,66... | collective-permute-start | bytes 479240 | tf_op jit(solution)/shard_map/ppermute | solution.py:17
  307.0 3.0 collective-permute-start.11
  318.1 4.5 collective-permute-start.12
  322.6 4.6 collective-permute-start.13
  327.2 6.8 %collective-permute-start.14 = (bf16[2,64,3,1]{1,3,2,0:T(2,128)(2,1)S(1)}, bf16[2,64,3,1]{1,3,2,0:T(2,128)(2,1)S(1)}, u32[]{:S(2)}, u32[]{:S(2)}) collective-permute-start(bf16[2,64,3,1]{1,3,2,0:T(2,128)(2,1)S(1)} %pad_maximum_fusion.19), channel_id=1, source_target_pairs={{60,0},{0,4},{4,8},{8,12},{12,16},{16,20},{20,24},{24,28},{28,32},... | collective-permute-start | bytes 2312 | tf_op jit(solution)/shard_map/ppermute | solution.py:23
Sparse Core Ops, SparseCore 0:
  10.4 56.1 all-gather.2
  347.1 269.2 all-reduce.1
where the time goes:
time: 635 us; the launch traced here: 632 us
  waiting for transfers between devices  354 us (56%)
  local copies, waits for them, and re-layouts  210 us (33%)
  starting transfers between devices  40.1 us (6%)
  between operations  14.5 us (2%)
  matrix products  12.2 us (2%)
    psum x1, waiting for transfers between devices, body(): lax.psum(to_atoms(local, channels, atoms) * scale, ('lat', 'lon', 'tm'))  269 us
    reshape x1, local copies, waits for them, and re-layouts, body(): gathered.reshape(atoms, 2, channels, 2, 4, 2, 4)  89.3 us
    transpose x1, local copies, waits for them, and re-layouts, body(): blocks = gathered.reshape(atoms, 2, channels, 2, 4, 2, 4).transpose(1, 3,...  86.1 us
    all_gather x1, waiting for transfers between devices, body(): gathered = lax.all_gather(dictionary, 'lon', axis=0, tiled=True)  38.2 us
    ppermute x10, starting transfers between devices, passed_along(): return lax.ppermute(shard, axis, pairs)  33 us
    ppermute x10, waiting for transfers between devices, passed_along(): return lax.ppermute(shard, axis, pairs)  25.1 us
    ppermute x5, waiting for transfers between devices, shifted(): return lax.ppermute(block, axis, route)  20.1 us
  transfers between devices with their start and end apart: 17, of which 17 were waited for; matrix products, arithmetic and copies ran while one was open for 1% of the time, Pallas kernels for 0%

commit v1 on v0

v1 whole, which is shorter than its diff:
```python
import math

import jax
import jax.numpy as jnp
from jax import lax
from jax.experimental import pallas as pl
from jax.experimental.pallas import tpu as pltpu
from jax.sharding import PartitionSpec as P

ITERS = 2
STEP_SIZE = 0.5
F32 = jnp.float32
BF16 = jnp.bfloat16
GROUP = ("lat", "tm")
COMBOS = [(h, a, b) for h in (0, 1) for a in (0, 1) for b in (0, 1)]
MAIN = 1024
LANES = 1280
HALF = 320
PACK = 416


def iota(shape, dim):
    return lax.broadcasted_iota(jnp.int32, shape, dim)


def dot(a, b):
    return jnp.dot(a, b, preferred_element_type=F32)


def dot_t(a, b):
    return lax.dot_general(a, b, (((1,), (1,)), ((), ())), preferred_element_type=F32)


def onehot(test):
    return jnp.where(test, 1.0, 0.0).astype(BF16)


def three(x):
    high = x.astype(BF16)
    rest = x - high.astype(F32)
    middle = rest.astype(BF16)
    low = (rest - middle.astype(F32)).astype(BF16)
    return high, middle, low


def call(kernel, outs, name, scratch=(), smem=0, n_in=1):
    vmem = pl.BlockSpec(memory_space=pltpu.VMEM)
    specs = [pl.BlockSpec(memory_space=pltpu.SMEM)] * smem + [vmem] * (n_in - smem)
    shapes = [jax.ShapeDtypeStruct(s, d) for s, d in outs]
    return pl.pallas_call(
        kernel,
        out_shape=shapes if len(shapes) > 1 else shapes[0],
        in_specs=specs,
        out_specs=[vmem] * len(shapes) if len(shapes) > 1 else vmem,
        scratch_shapes=list(scratch),
        name=name,
        compiler_params=pltpu.CompilerParams(vmem_limit_bytes=48 * 1024 * 1024),
    )


def pack_kernel(x_ref, z_ref, out_ref):
    row, col = iota((128, 128), 0), iota((128, 128), 1)
    order = onehot(((row & 3) * 32 + (row >> 2)) == col)
    split = [dot(x_ref[r], order) for r in range(8)]
    lane = iota((80, 128), 1)
    high, middle, low = three(z_ref[...])
    first = jnp.concatenate([high.astype(F32), middle[:32].astype(F32)], axis=0)
    second = jnp.concatenate([middle[32:].astype(F32), low.astype(F32)], axis=0)
    codes = jnp.concatenate([first, second], axis=1).astype(BF16)
    for core in range(2):
        for v in range(4):
            piece = jnp.zeros((80, 128), F32)
            for u_lo in range(2):
                for p2 in range(2):
                    slot = u_lo * 2 + p2
                    source = split[p2 * 4 + core * 2 + u_lo]
                    by = ((slot - v) % 4) * 32
                    moved = pltpu.roll(source, by, 1) if by else source
                    piece = jnp.where((lane >> 5) == slot, moved, piece)
            piece = piece.astype(BF16)
            for z in range(2):
                for t in range(4):
                    out_ref[(2 * z + core) * 4 + t, v * 80 : v * 80 + 80, :] = piece
        for z in range(2):
            for t in range(4):
                out_ref[(2 * z + core) * 4 + t, HALF:PACK, :] = codes


def unpack_kernel(in_ref, main_ref, first_ref, last_ref, left_ref):
    lane = iota((PACK, 128), 1)
    for pair in range(8):
        even = in_ref[2 * pair].astype(F32)
        odd = in_ref[2 * pair + 1].astype(F32)
        lanes = slice(pair * 128, pair * 128 + 128)
        left_ref[0:PACK, lanes] = jnp.where(lane < 64, even, pltpu.roll(odd, 64, 1)).astype(BF16)
        left_ref[PACK : 2 * PACK, lanes] = jnp.where(lane < 64, pltpu.roll(even, 64, 1), odd).astype(BF16)
    for block in range(4):
        n = iota((1024, 256), 1) + block * 256
        source = (((n >> 1) & 3) * 4 + ((n >> 3) & 3)) * 64 + (n & 1) * 32 + (n >> 5)
        order = onehot(iota((1024, 256), 0) == source)
        main_ref[:, block * 256 : block * 256 + 256] = dot(left_ref[...], order).astype(BF16)
    first_ref[...] = main_ref[:, 0:128]
    last_ref[...] = main_ref[:, MAIN - 128 : MAIN]


def slice_kernel(place_ref, d_ref, out_ref, rows_ref):
    rows_ref[...] = jnp.zeros((512, 128), F32)
    for i in range(78):
        h, half = i // 39, i % 39
        part = d_ref[:, i * 128 : i * 128 + 128].astype(F32)
        for k in range(4):
            at = (k * 2 + h) * 64 + half
            rows_ref[at : at + 1, :] = part[k : k + 1, :]
    u, v = place_ref[0], place_ref[1]
    which = iota((8, 128), 0)
    want = (which >> 2) * 64 + ((which >> 1) & 1) * 32 + u * 8 + (which & 1) * 4 + v
    picked = dot_t(onehot(iota((8, 128), 1) == want), rows_ref[...].astype(BF16))
    lane = iota((4, 128), 1)
    result = [None] * 8
    for k in range(4):
        pair = picked[:, k * 128 : k * 128 + 128]
        turned = pltpu.roll(pair, 64, 1)
        result[k] = jnp.where(lane < 64, pair[0:4], turned[4:8])
        result[4 + k] = jnp.where(lane < 64, turned[0:4], pair[4:8])
    for h in range(2):
        for ab in range(4):
            for k in range(4):
                at = (h * 4 + ab) * 4 + k
                rows_ref[at : at + 1, :] = result[h * 4 + k][ab : ab + 1, :]
    sent = rows_ref[0:32, :].astype(BF16)
    for peer in range(16):
        out_ref[peer] = sent


def turn_kernel(in_ref, out_ref, rows_ref):
    for peer in range(16):
        part = in_ref[peer].astype(F32)
        for hab in range(8):
            at = hab * 64 + peer * 4
            rows_ref[at : at + 4, :] = part[hab * 4 : hab * 4 + 4, :]
    turned = rows_ref[...].T
    kept = jnp.concatenate([turned[0:40], turned[64:104]], axis=0).astype(BF16)
    for copy in range(8):
        out_ref[copy] = kept


def shifted_codes(codes, z_ref):
    lane = iota((1, LANES), 1)
    t, p = (lane >> 3) & 3, lane & 7
    for index, (h, a, b) in enumerate(COMBOS):
        by = 32 * b + 8 * h + a
        moved = pltpu.roll(codes, by, 1) if by else codes
        kept = jnp.where((t >= h) & (p >= a), moved, 0.0)
        z_ref[index * 64 : index * 64 + 64, :] = kept.astype(BF16)


def partial_adjoint(b_ref, bt_ref, x_ref, east_ref, west_ref, z_ref, r_ref, u_ref):
    for chunk in range(5):
        lanes = slice(chunk * 256, chunk * 256 + 256)
        z = z_ref[:, lanes]
        for u_lo in range(2):
            rows = slice(u_lo * HALF, u_lo * HALF + HALF)
            held = slice(u_lo * PACK, u_lo * PACK + HALF)
            if chunk < 4:
                x = x_ref[held, lanes]
            else:
                x = jnp.concatenate([east_ref[held, :], west_ref[held, :]], axis=1)
            r_ref[rows, :] = (dot(b_ref[rows, :], z) - x.astype(F32)).astype(BF16)
        u_ref[:, lanes] = dot(bt_ref[...], r_ref[...])
    lane = iota((1, LANES), 1)
    t, p = (lane >> 3) & 3, lane & 7
    total = u_ref[0:64, :]
    for index, (h, a, b) in enumerate(COMBOS[1:], 1):
        moved = pltpu.roll(u_ref[index * 64 : index * 64 + 64, :], LANES - (32 * b + 8 * h + a), 1)
        total = total + jnp.where((t < 4 - h) & (p < 8 - a), moved, 0.0)
    return total


def first_kernel(b_in, x_ref, east_ref, west_ref, sum_ref, y_ref, bt_ref, b_ref, z_ref, r_ref, u_ref):
    for j in range(8):
        b_ref[j * 80 : j * 80 + 80, :] = b_in[j]
    bt_ref[...] = b_ref[...].T

    def rows_of(start, count):
        part = slice(start, start + count)
        return jnp.concatenate([x_ref[part, :], east_ref[part, :], west_ref[part, :]], axis=1).astype(F32)

    high = rows_of(HALF, 64)
    middle = jnp.concatenate([rows_of(HALF + 64, 32), rows_of(PACK + HALF, 32)], axis=0)
    low = rows_of(PACK + HALF + 32, 64)
    codes = (high + middle) + low
    y_ref[...] = codes
    shifted_codes(codes, z_ref)
    sum_ref[...] = partial_adjoint(b_ref, bt_ref, x_ref, east_ref, west_ref, z_ref, r_ref, u_ref)


def shrunk(moving, gradient, shrink):
    descent = moving - STEP_SIZE * gradient
    size = jnp.maximum(jnp.abs(descent) - shrink, 0.0)
    return jnp.where(descent < 0.0, -size, size)


def middle_kernel(factor, mine_ref, other_ref, moving_ref, current_ref, limit_ref, bt_ref, b_in, x_ref, east_ref, west_ref, sum_ref, y_ref, now_ref, b_ref, z_ref, r_ref, u_ref):
    for j in range(8):
        b_ref[j * 80 : j * 80 + 80, :] = b_in[j]
    updated = shrunk(moving_ref[...], mine_ref[...] + other_ref[...], STEP_SIZE * limit_ref[...])
    moving = updated + factor * (updated - current_ref[...])
    now_ref[...] = updated
    y_ref[...] = moving
    shifted_codes(moving, z_ref)
    sum_ref[...] = partial_adjoint(b_ref, bt_ref, x_ref, east_ref, west_ref, z_ref, r_ref, u_ref)


def last_kernel(scale, place_ref, mine_ref, other_ref, moving_ref, limit_ref, b_in, x_ref, codes_ref, grad_ref, z_ref):
    codes = shrunk(moving_ref[...], mine_ref[...] + other_ref[...], STEP_SIZE * limit_ref[...])
    core, z, t = place_ref[0], place_ref[1], place_ref[2]
    own = iota((MAIN, 128), 1)
    source = (own & 31) * 32 + t * 8 + (2 * z + core) * 2 + ((own >> 5) & 1)
    order = onehot((iota((MAIN, 128), 0) == source) & (own < 64))
    high, middle, low = three(codes[:, 0:MAIN])
    codes_ref[...] = (dot(high, order) + dot(middle, order)) + dot(low, order)
    shifted_codes(codes, z_ref)
    z_main = z_ref[:, 0:MAIN]
    x = x_ref[pl.ds(pl.multiple_of(z * PACK + t * 80, 16), 80), :]
    residual = (dot(b_in[z * 4 + t], z_main) - x.astype(F32)).astype(BF16)
    filled = jnp.concatenate([residual, jnp.zeros((48, MAIN), BF16)], axis=0)
    grad = dot_t(z_main, filled) * scale
    for peer in range(16):
        for hab in range(8):
            at = hab * 64 + peer * 4
            grad_ref[peer, hab * 4 : hab * 4 + 4, :] = grad[at : at + 4, :]


def add_kernel(in_ref, out_ref):
    total = in_ref[0]
    for peer in range(1, 16):
        total = total + in_ref[peer]
    for copy in range(16):
        out_ref[copy] = total


def place_kernel(in_ref, out_ref, rows_ref):
    for k in range(4):
        for h in range(2):
            for ab in range(4):
                a, b = ab // 2, ab % 2
                for z in range(2):
                    for core in range(2):
                        for t in range(4):
                            at = a * 32 + (2 * core + z) * 8 + b * 4 + t
                            row = (h * 4 + ab) * 4 + k
                            rows_ref[at : at + 1, :] = in_ref[(2 * z + core) * 4 + t, row : row + 1, :]
            even = rows_ref[...]
            odd = pltpu.roll(even, 88, 1)
            turned = jnp.concatenate([even, odd], axis=0).T
            for i in range(39):
                lanes = slice((h * 39 + i) * 128, (h * 39 + i) * 128 + 128)
                out_ref[k : k + 1, lanes] = turned[i : i + 1, :]


def body(signal, dictionary, codes_init, thresholds):
    lat, tm = lax.axis_index("lat"), lax.axis_index("tm")
    z, core = lat // 2, lat % 2
    place = jnp.stack([core, z, tm]).astype(jnp.int32)
    lon = lax.axis_size("lon")
    same_core = [[(2 * i + c) * 4 + t for i in range(2) for t in range(4)] for c in range(2)]

    sliced = call(slice_kernel, [((16, 32, 128), BF16)], "dict_slice", [pltpu.VMEM((512, 128), F32)], 1, 2)(
        jnp.stack([2 * core + z, tm]).astype(jnp.int32), dictionary
    )
    rows = signal[0].reshape(39, 2, 8, 128).transpose(2, 1, 0, 3)
    rows = jnp.pad(rows, ((0, 0), (0, 0), (0, 1), (0, 0))).reshape(8, 80, 128)
    packed = call(pack_kernel, [((16, PACK, 128), BF16)], "pack", n_in=2)(rows, codes_init[0].reshape(64, 64))
    arrived = lax.all_to_all(packed, GROUP, 0, 0, tiled=True)
    sliced = lax.all_to_all(sliced, "lon", 0, 0, tiled=True)
    turned = call(turn_kernel, [((8, 80, 512), BF16)], "dict_turn", [pltpu.VMEM((512, 128), F32)])(sliced)
    blocks = lax.all_to_all(turned, GROUP, 0, 0, tiled=True, axis_index_groups=same_core)
    x, first, last = call(
        unpack_kernel,
        [((2 * PACK, MAIN), BF16), ((2 * PACK, 128), BF16), ((2 * PACK, 128), BF16)],
        "unpack",
        [pltpu.VMEM((2 * PACK, MAIN), BF16)],
    )(arrived)
    east = lax.ppermute(first, "lon", [(i, (i - 1) % lon) for i in range(lon)])
    west = lax.ppermute(last, "lon", [(i, (i + 1) % lon) for i in range(lon)])

    work = [
        pltpu.VMEM((640, 512), BF16),
        pltpu.VMEM((512, LANES), BF16),
        pltpu.VMEM((640, 256), BF16),
        pltpu.VMEM((512, LANES), F32),
    ]
    state = ((64, LANES), F32)
    limits = thresholds.reshape(64, 1)
    mine, moving, blocks_t = call(
        first_kernel, [state, state, ((512, 640), BF16)], "first", work, n_in=4
    )(blocks, x, east, west)
    swap = [(i, i ^ 1) for i in range(4)]
    current = moving
    momentum_now = 1.0
    for turn in range(ITERS - 1):
        other = lax.ppermute(mine, "lat", swap)
        momentum_next = (1.0 + math.sqrt(1.0 + 4.0 * momentum_now * momentum_now)) / 2.0
        factor = (momentum_now - 1.0) / momentum_next
        momentum_now = momentum_next

        def step(*refs):
            middle_kernel(factor, *refs)

        mine, moving, current = call(step, [state, state, state], "middle", work, n_in=10)(
            mine, other, moving, current, limits, blocks_t, blocks, x, east, west
        )
    other = lax.ppermute(mine, "lat", swap)
    positions = lax.axis_size("tm") * lax.axis_size("lat") * lon * 64

    def ending(*refs):
        last_kernel(1.0 / math.sqrt(positions), *refs)

    codes, grad = call(
        ending, [((64, 128), F32), ((16, 32, 128), F32)], "last", [pltpu.VMEM((512, LANES), BF16)], 1, 7
    )(place, mine, other, moving, limits, blocks, x)
    grad = lax.all_to_all(grad, "lon", 0, 0, tiled=True)
    summed = call(add_kernel, [((16, 32, 128), F32)], "add")(grad)
    summed = lax.all_to_all(summed, GROUP, 0, 0, tiled=True)
    gradient = call(place_kernel, [((4, 9984), F32)], "place", [pltpu.VMEM((64, 128), F32)])(summed)
    return codes[:, :64].reshape(1, 64, 2, 32), gradient


def solution(mesh):
    placed = (P("tm", None, "lat", "lon"), P("lon", None), P("tm", None, "lat", "lon"), P())
    return jax.shard_map(
        body,
        mesh=mesh,
        in_specs=placed,
        out_specs=(P("tm", None, "lat", "lon"), P("lon", None)),
        check_vma=False,
    )
```

time: 635 us -> 125 us (0.20)
  waiting for transfers between devices: 354 us -> 44.8 us
  local copies, waits for them, and re-layouts: 210 us -> 8.12 us
  Pallas kernels: 0 us -> 15.8 us
  between operations: 14.5 us -> 0.74 us
  blocking collectives: 0 us -> 13.3 us
  matrix products: 12.2 us -> 0 us
    psum x1 -> x0, waiting for transfers between devices: 269 us -> none  [body(): lax.psum(to_atoms(local, channels, atoms) * scale, ('lat', 'lon', 'tm'))]
    reshape x6 -> x1, local copies, waits for them, and re-layouts: 96.7 us -> 0.1 us  [body(): limits = thresholds.reshape(64, 1)]
    transpose x2 -> x0, local copies, waits for them, and re-layouts: 88.9 us -> none  [the longest x1 86.1 us: body(): blocks = gathered.reshape(atoms, 2, channels, 2, 4, 2, 4).transpose(1, 3,...]
    ppermute x15 -> x4, waiting for transfers between devices: 45.2 us -> 3.77 us  [the longest x2 2.47 us: body(): other = lax.ppermute(mine, 'lat', swap)]
    all_to_all x0 -> x4, waiting for transfers between devices: none -> 41.1 us  [the longest x1 20.6 us: body(): arrived = lax.all_to_all(packed, GROUP, 0, 0, tiled=True)]
    all_gather x1 -> x0, waiting for transfers between devices: 38.2 us -> none  [body(): gathered = lax.all_gather(dictionary, 'lon', axis=0, tiled=True)]
    all_to_all x0 -> x4, starting transfers between devices: none -> 33.2 us  [the longest x1 11.7 us: body(): sliced = lax.all_to_all(sliced, 'lon', 0, 0, tiled=True)]
    ppermute x15 -> x4, starting transfers between devices: 40.1 us -> 8.46 us  [the longest x2 6.92 us: body(): other = lax.ppermute(mine, 'lat', swap)]
  transfers between devices with their start and end apart: 17 -> 8, of which waited for: 17 -> 7; matrix products, arithmetic and copies ran while one was open for 1% -> 2% of each run, Pallas kernels for 0% -> 4%
where the time goes in v1:
time: 125 us
  waiting for transfers between devices  44.8 us (36%)
  starting transfers between devices  41.7 us (33%)
  Pallas kernels  15.8 us (13%)
  blocking collectives  13.3 us (11%)
  local copies, waits for them, and re-layouts  8.12 us (6%)
    all_to_all x1, waiting for transfers between devices, body(): arrived = lax.all_to_all(packed, GROUP, 0, 0, tiled=True)  20.6 us
    all_to_all x1, blocking collectives, body(): grad = lax.all_to_all(grad, 'lon', 0, 0, tiled=True)  13.3 us
    all_to_all x1, starting transfers between devices, body(): sliced = lax.all_to_all(sliced, 'lon', 0, 0, tiled=True)  11.7 us
    all_to_all x1, starting transfers between devices, body(): summed = lax.all_to_all(summed, GROUP, 0, 0, tiled=True)  9.58 us
    all_to_all x1, waiting for transfers between devices, body(): lax.all_to_all(turned, GROUP, 0, 0, tiled=True, axis_index_groups=same_core)  7.91 us
    all_to_all x1, starting transfers between devices, body(): arrived = lax.all_to_all(packed, GROUP, 0, 0, tiled=True)  6.96 us
    ppermute x2, starting transfers between devices, body(): other = lax.ppermute(mine, 'lat', swap)  6.92 us
    all_to_all x1, waiting for transfers between devices, body(): summed = lax.all_to_all(summed, GROUP, 0, 0, tiled=True)  6.74 us
  transfers between devices with their start and end apart: 8, of which 7 were waited for; matrix products, arithmetic and copies ran while one was open for 2% of the time, Pallas kernels for 4%

profile of v1, /device:TPU:1, one launch (start us, length us, event | category | flops | bytes accessed | tf_op | source)
XLA Modules:
  0.0 124.6 jit_solution(4245339787664750385)
XLA Ops:
  0.7 0.9 copy-done.4
  1.6 1.5 %dict_slice.1 = bf16[16,32,128]{2,1,0:T(8,128)(2,1)} custom-call(s32[2]{0:T(128)S(1)} %pad_add_fusion.1.place_ref, bf16[4,9984]{1,0:T(4,128)(2,1)S(1)} %copy-done.4), custom_call_target="tpu_custom_call" | custom-call | tf_op jit(solution)/shard_map/dict_slice/pallas_call | solution.py:268
  3.1 11.7 %all-to-all-start = ((bf16[16,32,128]{2,1,0:T(8,128)(2,1)}), bf16[16,32,128]{2,1,0:T(8,128)(2,1)S(1)}, u32[]{:S(2)}, u32[]{:S(2)}) async-start(bf16[16,32,128]{2,1,0:T(8,128)(2,1)} %dict_slice.1), calls=%async_computation | async-start | bytes 262144 | tf_op jit(solution)/shard_map/all_to_all | solution.py:275
  14.9 0.8 copy.12.z_ref
  15.7 1.0 copy.17
  16.7 1.6 %pack.1 = bf16[16,416,128]{2,1,0:T(8,128)(2,1)} custom-call(bf16[8,80,128]{2,1,0:T(8,128)(2,1)S(1)} %bitcast.13, f32[64,64]{1,0:T(8,128)S(1)} %copy.12.z_ref), custom_call_target="tpu_custom_call" | custom-call | tf_op jit(solution)/shard_map/pack/pallas_call | solution.py:273
  18.3 5.8 %all-to-all-done.in_ref = bf16[16,32,128]{2,1,0:T(8,128)(2,1)S(1)} async-done(((bf16[16,32,128]{2,1,0:T(8,128)(2,1)}), bf16[16,32,128]{2,1,0:T(8,128)(2,1)S(1)}, u32[]{:S(2)}, u32[]{:S(2)}) %all-to-all-start) | async-done | bytes 131104 | tf_op jit(solution)/shard_map/all_to_all | solution.py:275
  24.1 7.0 %all-to-all-start.2 = ((bf16[16,416,128]{2,1,0:T(8,128)(2,1)}), bf16[16,416,128]{2,1,0:T(8,128)(2,1)S(1)}, u32[]{:S(2)}, u32[]{:S(2)}) async-start(bf16[16,416,128]{2,1,0:T(8,128)(2,1)} %pack.1), calls=%async_computation.2 | async-start | bytes 3407872 | tf_op jit(solution)/shard_map/all_to_all | solution.py:274
  31.1 1.0 dict_turn.1
  32.1 20.6 %all-to-all-done.2.in_ref = bf16[16,416,128]{2,1,0:T(8,128)(2,1)S(1)} async-done(((bf16[16,416,128]{2,1,0:T(8,128)(2,1)}), bf16[16,416,128]{2,1,0:T(8,128)(2,1)S(1)}, u32[]{:S(2)}, u32[]{:S(2)}) %all-to-all-start.2) | async-done | bytes 1703968 | tf_op jit(solution)/shard_map/all_to_all | solution.py:274
  52.7 1.2 copy-done
  53.9 4.9 %all-to-all-start.1 = ((bf16[8,80,512]{2,1,0:T(8,128)(2,1)}), bf16[8,80,512]{2,1,0:T(8,128)(2,1)S(1)}, u32[]{:S(2)}, u32[]{:S(2)}) async-start(bf16[8,80,512]{2,1,0:T(8,128)(2,1)} %dict_turn.1), calls=%async_computation.1 | async-start | bytes 1310720 | tf_op jit(solution)/shard_map/all_to_all | solution.py:277
  58.8 1.4 %copy-done.1 = bf16[16,416,128]{2,1,0:T(8,128)(2,1)S(1)} copy-done((bf16[16,416,128]{2,1,0:T(8,128)(2,1)S(1)}, bf16[16,416,128]{2,1,0:T(8,128)(2,1)}, u32[]{:S(2)}) %copy-start.1) | copy-done | bytes 1703960
  60.3 2.2 %unpack.1 = (bf16[832,1024]{1,0:T(8,128)(2,1)S(1)}, bf16[832,128]{1,0:T(8,128)(2,1)S(1)}, bf16[832,128]{1,0:T(8,128)(2,1)S(1)}) custom-call(bf16[16,416,128]{2,1,0:T(8,128)(2,1)S(1)} %copy-done.1), custom_call_target="tpu_custom_call" | custom-call | tf_op jit(solution)/shard_map/unpack/pallas_call | solution.py:278
  62.5 0.7 collective-permute-start
  63.3 0.8 collective-permute-start.1
  64.1 7.9 %all-to-all-done.1.b_in.refs_6_.refs_5_ = bf16[8,80,512]{2,1,0:T(8,128)(2,1)S(1)} async-done(((bf16[8,80,512]{2,1,0:T(8,128)(2,1)}), bf16[8,80,512]{2,1,0:T(8,128)(2,1)S(1)}, u32[]{:S(2)}, u32[]{:S(2)}) %all-to-all-start.1) | async-done | bytes 655392 | tf_op jit(solution)/shard_map/all_to_all | solution.py:277
  72.0 1.3 %collective-permute-done.1.west_ref.refs_9_ = bf16[832,128]{1,0:T(8,128)(2,1)S(1)} collective-permute-done((bf16[832,128]{1,0:T(8,128)(2,1)S(1)}, bf16[832,128]{1,0:T(8,128)(2,1)S(1)}, u32[]{:S(2)}, u32[]{:S(2)}) %collective-permute-start.1) | collective-permute-done | bytes 213024 | tf_op jit(solution)/shard_map/ppermute | solution.py:285
  73.3 2.5 %first.1 = (f32[64,1280]{1,0:T(8,128)S(1)}, f32[64,1280]{1,0:T(8,128)S(1)}, bf16[512,640]{1,0:T(8,128)(2,1)S(1)}) custom-call(bf16[8,80,512]{2,1,0:T(8,128)(2,1)S(1)} %all-to-all-done.1.b_in.refs_6_.refs_5_, bf16[832,1024]{1,0:T(8,128)(2,1)S(1)} %get-tuple-element.12.x_ref.refs_7_.refs_6_, bf16[832,128]{1,0:T(8,128)(2,1)S(1)} %collective-permute-done.east_ref.refs_8_, ...), custom_call_target="tpu_custom_call" | custom-call | tf_op jit(solution)/shard_map/first/pallas_call | solution.py:295
  75.8 0.8 copy-done.2
  76.7 6.5 %collective-permute-start.2 = (f32[64,1280]{1,0:T(8,128)S(1)}, f32[64,1280]{1,0:T(8,128)}, u32[]{:S(2)}, u32[]{:S(2)}) collective-permute-start(f32[64,1280]{1,0:T(8,128)S(1)} %get-tuple-element.15.refs_0_), channel_id=1, source_target_pairs={{0,64},{64,0},{128,192},{192,128},{1,65},{65,1},{129,193},{193,129... | collective-permute-start | bytes 983048 | tf_op jit(solution)/shard_map/ppermute | solution.py:302
  83.2 1.3 %collective-permute-done.2.refs_1_ = f32[64,1280]{1,0:T(8,128)} collective-permute-done((f32[64,1280]{1,0:T(8,128)S(1)}, f32[64,1280]{1,0:T(8,128)}, u32[]{:S(2)}, u32[]{:S(2)}) %collective-permute-start.2) | collective-permute-done | bytes 327712 | tf_op jit(solution)/shard_map/ppermute | solution.py:302
  84.5 1.1 copy-done.3
  85.6 3.6 %middle.1 = (f32[64,1280]{1,0:T(8,128)S(1)}, f32[64,1280]{1,0:T(8,128)S(1)}, f32[64,1280]{1,0:T(8,128)}) custom-call(f32[64,1280]{1,0:T(8,128)S(1)} %get-tuple-element.15.refs_0_, f32[64,1280]{1,0:T(8,128)} %collective-permute-done.2.refs_1_, f32[64,1280]{1,0:T(8,128)S(1)} %get-tuple-element.16.refs_2_.refs_3_, ...), custom_call_target="tpu_custom_call" | custom-call | tf_op jit(solution)/shard_map/middle/pallas_call | solution.py:310
  89.8 1.2 collective-permute-done.3.refs_2_
  91.0 1.5 %last.1 = (f32[64,128]{1,0:T(8,128)S(1)}, f32[16,32,128]{2,1,0:T(8,128)S(1)}) custom-call(s32[3]{0:T(128)S(1)} %pad_add_fusion.refs_0_, f32[64,1280]{1,0:T(8,128)S(1)} %get-tuple-element.18.refs_1_, f32[64,1280]{1,0:T(8,128)S(1)} %collective-permute-done.3.refs_2_, f32[64,1280]{1,0:T(8,128)S(1)} %get-tuple-element.19.refs_3_, f32[64,1]{1,0:T(8,128)S(1)} %copy.13.refs_4_, ...), custom_call_target="tpu_custom_call" | custom-call | tf_op jit(solution)/shard_map/last/pallas_call | solution.py:319
  92.5 13.3 %all_to_all.25.in_ref = f32[16,32,128]{2,1,0:T(8,128)S(1)} all-to-all(f32[16,32,128]{2,1,0:T(8,128)S(1)} %get-tuple-element.21), channel_id=1, replica_groups=mesh['lat'=4,'lon'=16,'tm'=4] {'lon'}, dimensions={0} | all-to-all | bytes 524288 | tf_op jit(solution)/shard_map/all_to_all | solution.py:322
  105.7 0.7 add.19
  106.5 9.6 %all-to-all-start.4 = ((f32[16,32,128]{2,1,0:T(8,128)}), f32[16,32,128]{2,1,0:T(8,128)S(1)}, u32[]{:S(2)}, u32[]{:S(2)}) async-start(f32[16,32,128]{2,1,0:T(8,128)} %add.19), calls=%async_computation.4 | async-start | bytes 524288 | tf_op jit(solution)/shard_map/all_to_all | solution.py:324
  116.1 0.7 copy.15
  116.8 6.7 %all-to-all-done.4.in_ref = f32[16,32,128]{2,1,0:T(8,128)S(1)} async-done(((f32[16,32,128]{2,1,0:T(8,128)}), f32[16,32,128]{2,1,0:T(8,128)S(1)}, u32[]{:S(2)}, u32[]{:S(2)}) %all-to-all-start.4) | async-done | bytes 262176 | tf_op jit(solution)/shard_map/all_to_all | solution.py:324
  123.5 1.1 place.1
  (13 shorter events, 0.7 us)
Async XLA Ops:
  0.7 0.9 copy-start.4
  3.1 21.0 %all-to-all-start = ((bf16[16,32,128]{2,1,0:T(8,128)(2,1)}), bf16[16,32,128]{2,1,0:T(8,128)(2,1)S(1)}, u32[]{:S(2)}, u32[]{:S(2)}) async-start(bf16[16,32,128]{2,1,0:T(8,128)(2,1)} %dict_slice.1), calls=%async_computation | async-start | bytes 262144 | tf_op jit(solution)/shard_map/all_to_all | solution.py:275
  24.1 28.6 %all-to-all-start.2 = ((bf16[16,416,128]{2,1,0:T(8,128)(2,1)}), bf16[16,416,128]{2,1,0:T(8,128)(2,1)S(1)}, u32[]{:S(2)}, u32[]{:S(2)}) async-start(bf16[16,416,128]{2,1,0:T(8,128)(2,1)} %pack.1), calls=%async_computation.2 | async-start | bytes 3407872 | tf_op jit(solution)/shard_map/all_to_all | solution.py:274
  52.7 1.2 copy-start
  53.9 18.1 %all-to-all-start.1 = ((bf16[8,80,512]{2,1,0:T(8,128)(2,1)}), bf16[8,80,512]{2,1,0:T(8,128)(2,1)S(1)}, u32[]{:S(2)}, u32[]{:S(2)}) async-start(bf16[8,80,512]{2,1,0:T(8,128)(2,1)} %dict_turn.1), calls=%async_computation.1 | async-start | bytes 1310720 | tf_op jit(solution)/shard_map/all_to_all | solution.py:277
  58.8 1.5 %copy-start.1 = (bf16[16,416,128]{2,1,0:T(8,128)(2,1)S(1)}, bf16[16,416,128]{2,1,0:T(8,128)(2,1)}, u32[]{:S(2)}) copy-start(bf16[16,416,128]{2,1,0:T(8,128)(2,1)} %copy-done) | copy-start | bytes 5111812
  62.5 20.6 %copy-start.5 = (f32[64]{0:T(128)S(1)}, f32[64]{0:T(128)}, u32[]{:S(2)}) copy-start(f32[64]{0:T(128)} %param.7) | copy-start | bytes 772
  62.5 9.5 %collective-permute-start = (bf16[832,128]{1,0:T(8,128)(2,1)S(1)}, bf16[832,128]{1,0:T(8,128)(2,1)S(1)}, u32[]{:S(2)}, u32[]{:S(2)}) collective-permute-start(bf16[832,128]{1,0:T(8,128)(2,1)S(1)} %get-tuple-element.13), channel_id=1, source_target_pairs={{0,60},{4,0},{8,4},{12,8},{16,12},{20,16},{24,20},{28,24},{32,28},... | collective-permute-start | bytes 638984 | tf_op jit(solution)/shard_map/ppermute | solution.py:284
  63.3 10.0 %collective-permute-start.1 = (bf16[832,128]{1,0:T(8,128)(2,1)S(1)}, bf16[832,128]{1,0:T(8,128)(2,1)S(1)}, u32[]{:S(2)}, u32[]{:S(2)}) collective-permute-start(bf16[832,128]{1,0:T(8,128)(2,1)S(1)} %get-tuple-element.14), channel_id=1, source_target_pairs={{0,4},{4,8},{8,12},{12,16},{16,20},{20,24},{24,28},{28,32},{32,36}... | collective-permute-start | bytes 638984 | tf_op jit(solution)/shard_map/ppermute | solution.py:285
  75.8 0.9 copy-start.2
  76.7 7.8 %collective-permute-start.2 = (f32[64,1280]{1,0:T(8,128)S(1)}, f32[64,1280]{1,0:T(8,128)}, u32[]{:S(2)}, u32[]{:S(2)}) collective-permute-start(f32[64,1280]{1,0:T(8,128)S(1)} %get-tuple-element.15.refs_0_), channel_id=1, source_target_pairs={{0,64},{64,0},{128,192},{192,128},{1,65},{65,1},{129,193},{193,129... | collective-permute-start | bytes 983048 | tf_op jit(solution)/shard_map/ppermute | solution.py:302
  84.5 1.1 copy-start.3
  89.2 1.7 %collective-permute-start.3 = (f32[64,1280]{1,0:T(8,128)S(1)}, f32[64,1280]{1,0:T(8,128)S(1)}, u32[]{:S(2)}, u32[]{:S(2)}) collective-permute-start(f32[64,1280]{1,0:T(8,128)S(1)} %get-tuple-element.18.refs_1_), channel_id=1, source_target_pairs={{0,64},{64,0},{128,192},{192,128},{1,65},{65,1},{129,193},{193,129... | collective-permute-start | bytes 983048 | tf_op jit(solution)/shard_map/ppermute | solution.py:313
  106.5 17.0 %all-to-all-start.4 = ((f32[16,32,128]{2,1,0:T(8,128)}), f32[16,32,128]{2,1,0:T(8,128)S(1)}, u32[]{:S(2)}, u32[]{:S(2)}) async-start(f32[16,32,128]{2,1,0:T(8,128)} %add.19), calls=%async_computation.4 | async-start | bytes 524288 | tf_op jit(solution)/shard_map/all_to_all | solution.py:324

commit v2 on v1

v2 whole, which is shorter than its diff:
```python
import math

import jax
import jax.numpy as jnp
from jax import lax
from jax.experimental import pallas as pl
from jax.experimental.pallas import tpu as pltpu
from jax.sharding import PartitionSpec as P


ITERS = 2
STEP_SIZE = 0.5
F32 = jnp.float32
BF16 = jnp.bfloat16
GROUP = ("lat", "tm")
COMBOS = [(h, a, b) for h in (0, 1) for a in (0, 1) for b in (0, 1)]
MAIN = 1024
LANES = 1280
HALF = 320
PACK = 384


def iota(shape, dim):
    return lax.broadcasted_iota(jnp.int32, shape, dim)


def dot(a, b):
    return jnp.dot(a, b, preferred_element_type=F32)


def dot_t(a, b):
    return lax.dot_general(a, b, (((1,), (1,)), ((), ())), preferred_element_type=F32)


def onehot(test):
    return jnp.where(test, 1.0, 0.0).astype(BF16)


def two(x):
    high = x.astype(BF16)
    return high, (x - high.astype(F32)).astype(BF16)


def three(x):
    high = x.astype(BF16)
    rest = x - high.astype(F32)
    middle = rest.astype(BF16)
    return high, middle, (rest - middle.astype(F32)).astype(BF16)


def call(kernel, outs, scratch=(), smem=0, n_in=1):
    vmem = pl.BlockSpec(memory_space=pltpu.VMEM)
    specs = [pl.BlockSpec(memory_space=pltpu.SMEM)] * smem + [vmem] * (n_in - smem)
    shapes = [jax.ShapeDtypeStruct(s, d) for s, d in outs]
    return pl.pallas_call(
        kernel,
        out_shape=shapes if len(shapes) > 1 else shapes[0],
        in_specs=specs,
        out_specs=[vmem] * len(shapes) if len(shapes) > 1 else vmem,
        scratch_shapes=list(scratch),
        compiler_params=pltpu.CompilerParams(vmem_limit_bytes=48 * 1024 * 1024),
    )


def pack_kernel(place_ref, x_ref, z_ref, own_ref, other_ref):
    row, col = iota((128, 128), 0), iota((128, 128), 1)
    order = onehot(((row & 3) * 32 + (row >> 2)) == col)
    lane = iota((80, 128), 1)
    high, low = two(z_ref[...])
    codes = jnp.concatenate([high, low], axis=1)
    for flip, out_ref in enumerate((own_ref, other_ref)):
        first = (place_ref[0] ^ flip) * 2
        split = [dot(x_ref[p2 * 4 + first + u_lo], order) for u_lo in range(2) for p2 in range(2)]
        for v in range(4):
            piece = jnp.zeros((80, 128), F32)
            for slot in range(4):
                by = ((slot - v) % 4) * 32
                moved = pltpu.roll(split[slot], by, 1) if by else split[slot]
                piece = jnp.where((lane >> 5) == slot, moved, piece)
            out_ref[v * 80 : v * 80 + 80, :] = piece.astype(BF16)
        out_ref[HALF:PACK, :] = codes


def unpack_kernel(place_ref, *refs):
    hours, (main_ref, first_ref, last_ref, left_ref) = refs[:4], refs[4:]
    lane = iota((PACK, 128), 1)
    for pair in range(8):
        even = hours[pair // 2][2 * (pair % 2)].astype(F32)
        odd = hours[pair // 2][2 * (pair % 2) + 1].astype(F32)
        lanes = slice(pair * 128, pair * 128 + 128)
        left_ref[0:PACK, lanes] = jnp.where(lane < 64, even, pltpu.roll(odd, 64, 1)).astype(BF16)
        left_ref[PACK : 2 * PACK, lanes] = jnp.where(lane < 64, pltpu.roll(even, 64, 1), odd).astype(BF16)
    lat, hour = 2 * place_ref[1] + place_ref[0], place_ref[2]
    for block in range(4):
        n = iota((1024, 256), 1) + block * 256
        slab = (((n >> 3) & 3) ^ hour) * 4 + (((n >> 1) & 3) ^ lat)
        source = slab * 64 + (n & 1) * 32 + (n >> 5)
        order = onehot(iota((1024, 256), 0) == source)
        main_ref[:, block * 256 : block * 256 + 256] = dot(left_ref[...], order).astype(BF16)
    first_ref[...] = main_ref[:, 0:128]
    last_ref[...] = main_ref[:, MAIN - 128 : MAIN]


def slice_kernel(place_ref, d_ref, out_ref, rows_ref):
    rows_ref[...] = jnp.zeros((512, 128), F32)
    for i in range(78):
        h, half = i // 39, i % 39
        part = d_ref[:, i * 128 : i * 128 + 128].astype(F32)
        for k in range(4):
            at = (k * 2 + h) * 64 + half
            rows_ref[at : at + 1, :] = part[k : k + 1, :]
    u, v = place_ref[0], place_ref[1]
    which = iota((8, 128), 0)
    want = (which >> 2) * 64 + ((which >> 1) & 1) * 32 + u * 8 + (which & 1) * 4 + v
    picked = dot_t(onehot(iota((8, 128), 1) == want), rows_ref[...].astype(BF16))
    lane = iota((4, 128), 1)
    result = [None] * 8
    for k in range(4):
        pair = picked[:, k * 128 : k * 128 + 128]
        turned = pltpu.roll(pair, 64, 1)
        result[k] = jnp.where(lane < 64, pair[0:4], turned[4:8])
        result[4 + k] = jnp.where(lane < 64, turned[0:4], pair[4:8])
    for h in range(2):
        for ab in range(4):
            for k in range(4):
                at = (h * 4 + ab) * 4 + k
                rows_ref[at : at + 1, :] = result[h * 4 + k][ab : ab + 1, :]
    sent = rows_ref[0:32, :].astype(BF16)
    for peer in range(16):
        out_ref[peer] = sent


def turn_kernel(in_ref, out_ref, rows_ref):
    for peer in range(16):
        part = in_ref[peer].astype(F32)
        for hab in range(8):
            at = hab * 64 + peer * 4
            rows_ref[at : at + 4, :] = part[hab * 4 : hab * 4 + 4, :]
    turned = rows_ref[...].T
    kept = jnp.concatenate([turned[0:40], turned[64:104]], axis=0).astype(BF16)
    for copy in range(8):
        out_ref[copy * 80 : copy * 80 + 80, :] = kept


def shifted_codes(codes, z_ref):
    lane = iota((1, LANES), 1)
    t, p = (lane >> 3) & 3, lane & 7
    for index, (h, a, b) in enumerate(COMBOS):
        by = 32 * b + 8 * h + a
        moved = pltpu.roll(codes, by, 1) if by else codes
        kept = jnp.where((t >= h) & (p >= a), moved, 0.0)
        z_ref[index * 64 : index * 64 + 64, :] = kept.astype(BF16)


def partial_adjoint(b_ref, bt_ref, x_ref, east_ref, west_ref, z_ref, r_ref, u_ref):
    for chunk in range(5):
        lanes = slice(chunk * 256, chunk * 256 + 256)
        z = z_ref[:, lanes]
        for u_lo in range(2):
            rows = slice(u_lo * HALF, u_lo * HALF + HALF)
            held = slice(u_lo * PACK, u_lo * PACK + HALF)
            if chunk < 4:
                x = x_ref[held, lanes]
            else:
                x = jnp.concatenate([east_ref[held, :], west_ref[held, :]], axis=1)
            r_ref[rows, :] = (dot(b_ref[rows, :], z) - x.astype(F32)).astype(BF16)
        u_ref[:, lanes] = dot(bt_ref[...], r_ref[...])
    lane = iota((1, LANES), 1)
    t, p = (lane >> 3) & 3, lane & 7
    total = u_ref[0:64, :]
    for index, (h, a, b) in enumerate(COMBOS[1:], 1):
        moved = pltpu.roll(u_ref[index * 64 : index * 64 + 64, :], LANES - (32 * b + 8 * h + a), 1)
        total = total + jnp.where((t < 4 - h) & (p < 8 - a), moved, 0.0)
    return total


def first_kernel(b_ref, x_ref, east_ref, west_ref, sum_ref, y_ref, bt_ref, z_ref, r_ref, u_ref):
    bt_ref[...] = b_ref[...].T

    def rows_of(start, count):
        part = slice(start, start + count)
        return jnp.concatenate([x_ref[part, :], east_ref[part, :], west_ref[part, :]], axis=1).astype(F32)

    codes = rows_of(HALF, 64) + rows_of(PACK + HALF, 64)
    y_ref[...] = codes
    shifted_codes(codes, z_ref)
    sum_ref[...] = partial_adjoint(b_ref, bt_ref, x_ref, east_ref, west_ref, z_ref, r_ref, u_ref)


def shrunk(moving, gradient, shrink):
    descent = moving - STEP_SIZE * gradient
    size = jnp.maximum(jnp.abs(descent) - shrink, 0.0)
    return jnp.where(descent < 0.0, -size, size)


def middle_kernel(factor, mine_ref, other_ref, moving_ref, current_ref, limit_ref, bt_ref, b_ref, x_ref, east_ref, west_ref, sum_ref, y_ref, now_ref, z_ref, r_ref, u_ref):
    updated = shrunk(moving_ref[...], mine_ref[...] + other_ref[...], STEP_SIZE * limit_ref[...])
    moving = updated + factor * (updated - current_ref[...])
    now_ref[...] = updated
    y_ref[...] = moving
    shifted_codes(moving, z_ref)
    sum_ref[...] = partial_adjoint(b_ref, bt_ref, x_ref, east_ref, west_ref, z_ref, r_ref, u_ref)


def last_kernel(scale, place_ref, mine_ref, other_ref, moving_ref, limit_ref, b_ref, x_ref, codes_ref, grad_ref, z_ref, g_ref):
    codes = shrunk(moving_ref[...], mine_ref[...] + other_ref[...], STEP_SIZE * limit_ref[...])
    core, z, t = place_ref[0], place_ref[1], place_ref[2]
    own = iota((MAIN, 128), 1)
    source = (own & 31) * 32 + t * 8 + (2 * z + core) * 2 + ((own >> 5) & 1)
    order = onehot((iota((MAIN, 128), 0) == source) & (own < 64))
    high, middle, low = three(codes[:, 0:MAIN])
    codes_ref[...] = (dot(high, order) + dot(middle, order)) + dot(low, order)
    shifted_codes(codes, z_ref)
    z_main = z_ref[:, 0:MAIN]
    x = x_ref[pl.ds(pl.multiple_of(z * PACK, 16), HALF), :]
    held = b_ref[pl.ds(pl.multiple_of(z * HALF, 16), HALF), :]
    residual = (dot(held, z_main) - x.astype(F32)).astype(BF16)
    g_ref[...] = dot_t(z_main, residual) * scale
    for peer in range(16):
        parts = [g_ref[hab * 64 + peer * 4 : hab * 64 + peer * 4 + 4, :] for hab in range(8)]
        grad_ref[peer] = jnp.concatenate(parts, axis=0).astype(BF16)


def add_kernel(in_ref, out_ref):
    total = in_ref[0].astype(F32)
    for peer in range(1, 16):
        total = total + in_ref[peer].astype(F32)
    out_ref[...] = total


def place_kernel(place_ref, own_ref, core_ref, z_ref, both_ref, out_ref, parts_ref, rows_ref):
    core, z = place_ref[0], place_ref[1]
    for flip, piece in enumerate((own_ref, core_ref, z_ref, both_ref)):
        u = 2 * (core ^ (flip & 1)) + (z ^ (flip >> 1))
        for v in range(4):
            low = v * 80 // 128 * 128
            turn = v * 80 - low
            lanes = piece[:, low : min(low + 256, HALF)]
            if lanes.shape[1] < 256:
                lanes = jnp.concatenate([lanes, jnp.zeros((32, 256 - lanes.shape[1]), F32)], axis=1)
            moved = pltpu.roll(lanes, 256 - turn, 1) if turn else lanes
            parts_ref[u * 4 + v] = moved[:, 0:128]
    for k in range(4):
        for h in range(2):
            for ab in range(4):
                row = (h * 4 + ab) * 4 + k
                for uv in range(16):
                    at = (ab // 2) * 32 + (uv // 4) * 8 + (ab % 2) * 4 + uv % 4
                    rows_ref[at : at + 1, :] = parts_ref[uv, row : row + 1, :]
            even = rows_ref[...]
            odd = pltpu.roll(even, 88, 1)
            turned = jnp.concatenate([even, odd], axis=0).T
            for i in range(39):
                lanes = slice((h * 39 + i) * 128, (h * 39 + i) * 128 + 128)
                out_ref[k : k + 1, lanes] = turned[i : i + 1, :]


def program(signal, dictionary, codes_init, thresholds):
    lat, tm = lax.axis_index("lat"), lax.axis_index("tm")
    z, core = lat // 2, lat % 2
    place = jnp.stack([core, z, tm]).astype(jnp.int32)
    lon = lax.axis_size("lon")
    same_core = [[(2 * i + c) * 4 + t for i in range(2) for t in range(4)] for c in range(2)]

    sliced = call(slice_kernel, [((16, 32, 128), BF16)], [pltpu.VMEM((512, 128), F32)], 1, 2)(
        jnp.stack([2 * core + z, tm]).astype(jnp.int32), dictionary
    )
    rows = signal[0].reshape(39, 2, 8, 128).transpose(2, 1, 0, 3)
    rows = jnp.pad(rows, ((0, 0), (0, 0), (0, 1), (0, 0))).reshape(8, 80, 128)
    kept, given = call(pack_kernel, [((PACK, 128), BF16)] * 2, (), 1, 3)(
        place, rows, codes_init[0].reshape(64, 64)
    )

    def flipped(block, axis, by):
        return lax.ppermute(block, axis, [(i, i ^ by) for i in range(4)])

    beside = flipped(given, "lat", 1)
    bands = [kept, beside, flipped(kept, "lat", 2), flipped(beside, "lat", 2)]
    hour = jnp.stack(bands)
    hours = [hour] + [flipped(hour, "tm", by) for by in (1, 2, 3)]
    sliced = lax.all_to_all(sliced, "lon", 0, 0, tiled=True)
    turned = call(turn_kernel, [((640, 512), BF16)], [pltpu.VMEM((512, 128), F32)])(sliced)
    blocks = lax.all_to_all(turned, GROUP, 0, 0, tiled=True, axis_index_groups=same_core)
    x, first, last = call(
        unpack_kernel,
        [((2 * PACK, MAIN), BF16), ((2 * PACK, 128), BF16), ((2 * PACK, 128), BF16)],
        [pltpu.VMEM((2 * PACK, MAIN), BF16)],
        1,
        5,
    )(place, *hours)
    east = lax.ppermute(first, "lon", [(i, (i - 1) % lon) for i in range(lon)])
    west = lax.ppermute(last, "lon", [(i, (i + 1) % lon) for i in range(lon)])

    work = [
        pltpu.VMEM((512, LANES), BF16),
        pltpu.VMEM((640, 256), BF16),
        pltpu.VMEM((512, LANES), F32),
    ]
    state = ((64, LANES), F32)
    limits = thresholds.reshape(64, 1)
    mine, moving, blocks_t = call(
        first_kernel, [state, state, ((512, 640), BF16)], work, n_in=4
    )(blocks, x, east, west)
    swap = [(i, i ^ 1) for i in range(4)]
    current = moving
    momentum_now = 1.0
    for _ in range(ITERS - 1):
        other = lax.ppermute(mine, "lat", swap)
        momentum_next = (1.0 + math.sqrt(1.0 + 4.0 * momentum_now * momentum_now)) / 2.0
        factor = (momentum_now - 1.0) / momentum_next
        momentum_now = momentum_next

        def step(*refs):
            middle_kernel(factor, *refs)

        mine, moving, current = call(step, [state, state, state], work, n_in=10)(
            mine, other, moving, current, limits, blocks_t, blocks, x, east, west
        )
    other = lax.ppermute(mine, "lat", swap)
    positions = lax.axis_size("tm") * lax.axis_size("lat") * lon * 64

    def ending(*refs):
        last_kernel(1.0 / math.sqrt(positions), *refs)

    codes, grad = call(
        ending,
        [((64, 128), F32), ((16, 32, HALF), BF16)],
        [pltpu.VMEM((512, LANES), BF16), pltpu.VMEM((512, HALF), F32)],
        1,
        7,
    )(place, mine, other, moving, limits, blocks, x)
    grad = lax.all_to_all(grad, "lon", 0, 0, tiled=True)
    summed = call(add_kernel, [((32, HALF), F32)])(grad)
    others = [lax.ppermute(summed, "lat", [(i, i ^ flip) for i in range(4)]) for flip in (1, 2, 3)]
    gradient = call(
        place_kernel,
        [((4, 9984), F32)],
        [pltpu.VMEM((16, 32, 128), F32), pltpu.VMEM((64, 128), F32)],
        1,
        5,
    )(place, summed, *others)
    return codes[:, :64].reshape(1, 64, 2, 32), gradient


def solution(mesh):
    placed = (P("tm", None, "lat", "lon"), P("lon", None), P("tm", None, "lat", "lon"), P())
    return jax.shard_map(
        program,
        mesh=mesh,
        in_specs=placed,
        out_specs=(P("tm", None, "lat", "lon"), P("lon", None)),
        check_vma=False,
    )
```

time: 125 us -> 120 us (0.960)
  blocking collectives: 13.3 us -> 40.2 us
  starting transfers between devices: 41.7 us -> 20.6 us
  waiting for transfers between devices: 44.8 us -> 37.6 us
  local copies, waits for them, and re-layouts: 8.12 us -> 3.77 us
    all_to_all x4 -> x1, waiting for transfers between devices: 41.1 us -> 0.01 us  [program(): lax.all_to_all(turned, GROUP, 0, 0, tiled=True, axis_index_groups=same_core)]
    ppermute x4 -> x13, waiting for transfers between devices: 3.77 us -> 37.6 us  [the longest x6 20.8 us: flipped(): return lax.ppermute(block, axis, [(i, i ^ by) for i in range(4)])]
    all_to_all x4 -> x1, starting transfers between devices: 33.2 us -> 4.39 us  [program(): lax.all_to_all(turned, GROUP, 0, 0, tiled=True, axis_index_groups=same_core)]
    all_to_all x1 -> x2, blocking collectives: 13.3 us -> 40.2 us  [the longest x1 20.8 us: program(): sliced = lax.all_to_all(sliced, 'lon', 0, 0, tiled=True)]
    ppermute x4 -> x13, starting transfers between devices: 8.46 us -> 16.2 us  [the longest x6 8.67 us: flipped(): return lax.ppermute(block, axis, [(i, i ^ by) for i in range(4)])]
    unnamed x12, local copies, waits for them, and re-layouts: 5.51 us -> 2.84 us
    another operation x2, local copies, waits for them, and re-layouts: 1.8 us -> 0.12 us  [the longest x1 0.07 us: program(): codes_init[0].reshape(64, 64)]
  transfers between devices with their start and end apart: 8 -> 14, of which waited for: 7 -> 8; matrix products, arithmetic and copies ran while one was open for 2% -> 1% of each run, Pallas kernels for 4% -> 3%
where the time goes in v2:
time: 120 us; the launch traced here: 118 us
  blocking collectives  40.2 us (34%)
  waiting for transfers between devices  37.6 us (31%)
  starting transfers between devices  20.6 us (17%)
  Pallas kernels  15.4 us (13%)
  local copies, waits for them, and re-layouts  3.77 us (3%)
    all_to_all x1, blocking collectives, program(): sliced = lax.all_to_all(sliced, 'lon', 0, 0, tiled=True)  20.8 us
    ppermute x6, waiting for transfers between devices, flipped(): return lax.ppermute(block, axis, [(i, i ^ by) for i in range(4)])  20.8 us
    all_to_all x1, blocking collectives, program(): grad = lax.all_to_all(grad, 'lon', 0, 0, tiled=True)  19.4 us
    ppermute x6, starting transfers between devices, flipped(): return lax.ppermute(block, axis, [(i, i ^ by) for i in range(4)])  8.67 us
    ppermute x1, waiting for transfers between devices, program(): east = lax.ppermute(first, 'lon', [(i, (i - 1) % lon) for i in range(lon)])  7.16 us
    ppermute x1, waiting for transfers between devices, program(): west = lax.ppermute(last, 'lon', [(i, (i + 1) % lon) for i in range(lon)])  5.17 us
    all_to_all x1, starting transfers between devices, program(): lax.all_to_all(turned, GROUP, 0, 0, tiled=True, axis_index_groups=same_core)  4.39 us
    pallas_call x1, Pallas kernels, program(): call(step, [state, state, state], work, n_in=10)  3.63 us
  transfers between devices with their start and end apart: 14, of which 8 were waited for; matrix products, arithmetic and copies ran while one was open for 1% of the time, Pallas kernels for 3%

profile of v2, /device:TPU:1, one launch (start us, length us, event | category | flops | bytes accessed | tf_op | source)
XLA Modules:
  0.0 118.5 jit_solution(3306599873624283033)
XLA Ops:
  0.7 0.9 copy-done.2
  1.6 0.9 shard_map.59
  2.5 20.8 %all_to_all.21.in_ref = bf16[16,32,128]{2,1,0:T(8,128)(2,1)S(1)} all-to-all(bf16[16,32,128]{2,1,0:T(8,128)(2,1)S(1)} %shard_map.59), channel_id=1, replica_groups=mesh['lat'=4,'lon'=16,'tm'=4] {'lon'}, dimensions={0} | all-to-all | bytes 262144 | tf_op jit(solution)/shard_map/all_to_all | solution.py:281
  23.3 1.0 shard_map.60
  24.3 4.4 %all-to-all-start.1 = ((bf16[8,80,512]{2,1,0:T(8,128)(2,1)}), bf16[8,80,512]{2,1,0:T(8,128)(2,1)S(1)}, u32[]{:S(2)}, u32[]{:S(2)}) async-start(bf16[8,80,512]{2,1,0:T(8,128)(2,1)} %bitcast.4), calls=%async_computation.1 | async-start | bytes 1310720 | tf_op jit(solution)/shard_map/all_to_all | solution.py:283
  28.9 0.9 shard_map.61
  29.8 2.6 %collective-permute-start = (bf16[384,128]{1,0:T(8,128)(2,1)S(1)}, bf16[384,128]{1,0:T(8,128)(2,1)S(1)}, u32[]{:S(2)}, u32[]{:S(2)}) collective-permute-start(bf16[384,128]{1,0:T(8,128)(2,1)S(1)} %get-tuple-element.15), channel_id=1, source_target_pairs={{0,64},{64,0},{128,192},{192,128},{1,65},{65,1},{129,193},{193,129... | collective-permute-start | bytes 294920 | tf_op jit(solution)/shard_map/ppermute | solution.py:275
  32.5 1.7 %collective-permute-start.1 = (bf16[384,128]{1,0:T(8,128)(2,1)S(1)}, bf16[384,128]{1,0:T(8,128)(2,1)S(1)}, u32[]{:S(2)}, u32[]{:S(2)}) collective-permute-start(bf16[384,128]{1,0:T(8,128)(2,1)S(1)} %get-tuple-element.14), channel_id=1, source_target_pairs={{0,128},{64,192},{128,0},{192,64},{1,129},{65,193},{129,1},{193,65... | collective-permute-start | bytes 294920 | tf_op jit(solution)/shard_map/ppermute | solution.py:275
  34.2 0.9 collective-permute-start.2
  35.2 2.5 %collective-permute-done.1 = bf16[384,128]{1,0:T(8,128)(2,1)S(1)} collective-permute-done((bf16[384,128]{1,0:T(8,128)(2,1)S(1)}, bf16[384,128]{1,0:T(8,128)(2,1)S(1)}, u32[]{:S(2)}, u32[]{:S(2)}) %collective-permute-start.1) | collective-permute-done | bytes 98336 | tf_op jit(solution)/shard_map/ppermute | solution.py:275
  37.7 2.1 %collective-permute-done.2 = bf16[384,128]{1,0:T(8,128)(2,1)S(1)} collective-permute-done((bf16[384,128]{1,0:T(8,128)(2,1)S(1)}, bf16[384,128]{1,0:T(8,128)(2,1)S(1)}, u32[]{:S(2)}, u32[]{:S(2)}) %collective-permute-start.2) | collective-permute-done | bytes 98336 | tf_op jit(solution)/shard_map/ppermute | solution.py:275
  39.9 2.6 %collective-permute-start.5 = (bf16[4,384,128]{2,1,0:T(8,128)(2,1)S(1)}, bf16[4,384,128]{2,1,0:T(8,128)(2,1)S(1)}, u32[]{:S(2)}, u32[]{:S(2)}) collective-permute-start(bf16[4,384,128]{2,1,0:T(8,128)(2,1)S(1)} %pad_maximum_fusion.refs_0_), channel_id=1, source_target_pairs={{0,3},{1,2},{2,1},{3,0},{4,7},{5,6},{6,5},{7,4},{8,11},{9,10},{10,... | collective-permute-start | bytes 1179656 | tf_op jit(solution)/shard_map/ppermute | solution.py:275
  42.5 0.6 collective-permute-start.4
  43.2 16.1 %collective-permute-done.5.refs_3_ = bf16[4,384,128]{2,1,0:T(8,128)(2,1)S(1)} collective-permute-done((bf16[4,384,128]{2,1,0:T(8,128)(2,1)S(1)}, bf16[4,384,128]{2,1,0:T(8,128)(2,1)S(1)}, u32[]{:S(2)}, u32[]{:S(2)}) %collective-permute-start.5) | collective-permute-done | bytes 393248 | tf_op jit(solution)/shard_map/ppermute | solution.py:275
  59.3 2.6 %shard_map.62 = (bf16[768,1024]{1,0:T(8,128)(2,1)S(1)}, bf16[768,128]{1,0:T(8,128)(2,1)S(1)}, bf16[768,128]{1,0:T(8,128)(2,1)S(1)}) custom-call(s32[3]{0:T(128)S(1)} %pad_add_fusion.place_ref.refs_0_, bf16[4,384,128]{2,1,0:T(8,128)(2,1)S(1)} %pad_maximum_fusion.refs_0_, bf16[4,384,128]{2,1,0:T(8,128)(2,1)S(1)} %collective-permute-done.3.refs_1_, ...), custom_call_target="tpu_custom_call" | custom-call | tf_op jit(solution)/shard_map/pallas_call | solution.py:284
  62.0 1.4 %collective-permute-start.6 = (bf16[768,128]{1,0:T(8,128)(2,1)S(1)}, bf16[768,128]{1,0:T(8,128)(2,1)S(1)}, u32[]{:S(2)}, u32[]{:S(2)}) collective-permute-start(bf16[768,128]{1,0:T(8,128)(2,1)S(1)} %get-tuple-element.17), channel_id=1, source_target_pairs={{0,60},{4,0},{8,4},{12,8},{16,12},{20,16},{24,20},{28,24},{32,28},... | collective-permute-start | bytes 589832 | tf_op jit(solution)/shard_map/ppermute | solution.py:291
  63.5 7.2 %collective-permute-done.6.east_ref.refs_8_ = bf16[768,128]{1,0:T(8,128)(2,1)S(1)} collective-permute-done((bf16[768,128]{1,0:T(8,128)(2,1)S(1)}, bf16[768,128]{1,0:T(8,128)(2,1)S(1)}, u32[]{:S(2)}, u32[]{:S(2)}) %collective-permute-start.6) | collective-permute-done | bytes 196640 | tf_op jit(solution)/shard_map/ppermute | solution.py:291
  70.7 5.2 %collective-permute-done.7.west_ref.refs_9_ = bf16[768,128]{1,0:T(8,128)(2,1)S(1)} collective-permute-done((bf16[768,128]{1,0:T(8,128)(2,1)S(1)}, bf16[768,128]{1,0:T(8,128)(2,1)S(1)}, u32[]{:S(2)}, u32[]{:S(2)}) %collective-permute-start.7) | collective-permute-done | bytes 196640 | tf_op jit(solution)/shard_map/ppermute | solution.py:292
  75.9 2.5 %shard_map.63 = (f32[64,1280]{1,0:T(8,128)S(1)}, f32[64,1280]{1,0:T(8,128)S(1)}, bf16[512,640]{1,0:T(8,128)(2,1)S(1)}) custom-call(bf16[640,512]{1,0:T(8,128)(2,1)S(1)} %bitcast.19, bf16[768,1024]{1,0:T(8,128)(2,1)S(1)} %get-tuple-element.16.x_ref.refs_7_.refs_6_, bf16[768,128]{1,0:T(8,128)(2,1)S(1)} %collective-permute-done.6.east_ref.refs_8_, ...), custom_call_target="tpu_custom_call" | custom-call | tf_op jit(solution)/shard_map/pallas_call | solution.py:301
  78.4 0.8 copy-done
  79.3 2.2 %collective-permute-start.8 = (f32[64,1280]{1,0:T(8,128)S(1)}, f32[64,1280]{1,0:T(8,128)}, u32[]{:S(2)}, u32[]{:S(2)}) collective-permute-start(f32[64,1280]{1,0:T(8,128)S(1)} %get-tuple-element.19.refs_0_), channel_id=1, source_target_pairs={{0,64},{64,0},{128,192},{192,128},{1,65},{65,1},{129,193},{193,129... | collective-permute-start | bytes 983048 | tf_op jit(solution)/shard_map/ppermute | solution.py:308
  81.6 1.3 %collective-permute-done.8.refs_1_ = f32[64,1280]{1,0:T(8,128)} collective-permute-done((f32[64,1280]{1,0:T(8,128)S(1)}, f32[64,1280]{1,0:T(8,128)}, u32[]{:S(2)}, u32[]{:S(2)}) %collective-permute-start.8) | collective-permute-done | bytes 327712 | tf_op jit(solution)/shard_map/ppermute | solution.py:308
  82.9 1.1 copy-done.1
  83.9 3.6 %shard_map.64 = (f32[64,1280]{1,0:T(8,128)S(1)}, f32[64,1280]{1,0:T(8,128)S(1)}, f32[64,1280]{1,0:T(8,128)}) custom-call(f32[64,1280]{1,0:T(8,128)S(1)} %get-tuple-element.19.refs_0_, f32[64,1280]{1,0:T(8,128)} %collective-permute-done.8.refs_1_, f32[64,1280]{1,0:T(8,128)S(1)} %get-tuple-element.20.refs_2_.refs_3_, ...), custom_call_target="tpu_custom_call" | custom-call | tf_op jit(solution)/shard_map/pallas_call | solution.py:316
  87.6 0.5 collective-permute-start.9
  88.0 1.3 %collective-permute-done.9.refs_2_ = f32[64,1280]{1,0:T(8,128)S(1)} collective-permute-done((f32[64,1280]{1,0:T(8,128)S(1)}, f32[64,1280]{1,0:T(8,128)S(1)}, u32[]{:S(2)}, u32[]{:S(2)}) %collective-permute-start.9) | collective-permute-done | bytes 327712 | tf_op jit(solution)/shard_map/ppermute | solution.py:319
  89.3 1.9 %shard_map.65 = (f32[64,128]{1,0:T(8,128)S(1)}, bf16[16,32,320]{2,1,0:T(8,128)(2,1)S(1)}) custom-call(s32[3]{0:T(128)S(1)} %pad_add_fusion.place_ref.refs_0_, f32[64,1280]{1,0:T(8,128)S(1)} %get-tuple-element.22.refs_1_, f32[64,1280]{1,0:T(8,128)S(1)} %collective-permute-done.9.refs_2_, f32[64,1280]{1,0:T(8,128)S(1)} %get-tuple-element.23.refs_3_, ...), custom_call_target="tpu_custom_call" | custom-call | tf_op jit(solution)/shard_map/pallas_call | solution.py:325
  91.2 19.4 %all_to_all.22.in_ref = bf16[16,32,320]{2,1,0:T(8,128)(2,1)S(1)} all-to-all(bf16[16,32,320]{2,1,0:T(8,128)(2,1)S(1)} %get-tuple-element.25), channel_id=1, replica_groups=mesh['lat'=4,'lon'=16,'tm'=4] {'lon'}, dimensions={0} | all-to-all | bytes 655360 | tf_op jit(solution)/shard_map/all_to_all | solution.py:332
  110.8 3.2 %collective-permute-start.11 = (f32[32,320]{1,0:T(8,128)S(1)}, f32[32,320]{1,0:T(8,128)S(1)}, u32[]{:S(2)}, u32[]{:S(2)}) collective-permute-start(f32[32,320]{1,0:T(8,128)S(1)} %shard_map.66.own_ref), channel_id=1, source_target_pairs={{0,128},{64,192},{128,0},{192,64},{1,129},{65,193},{129,1},{193,65... | collective-permute-start | bytes 122888 | tf_op jit(solution)/shard_map/ppermute | solution.py:334
  114.0 0.7 copy.15
  114.7 2.0 %collective-permute-done.11.z_ref = f32[32,320]{1,0:T(8,128)S(1)} collective-permute-done((f32[32,320]{1,0:T(8,128)S(1)}, f32[32,320]{1,0:T(8,128)S(1)}, u32[]{:S(2)}, u32[]{:S(2)}) %collective-permute-start.11) | collective-permute-done | bytes 40992 | tf_op jit(solution)/shard_map/ppermute | solution.py:334
  116.7 1.8 %shard_map.67 = f32[4,9984]{1,0:T(4,128)} custom-call(s32[3]{0:T(128)S(1)} %pad_add_fusion.place_ref.refs_0_, f32[32,320]{1,0:T(8,128)S(1)} %shard_map.66.own_ref, f32[32,320]{1,0:T(8,128)S(1)} %collective-permute-done.10.core_ref, f32[32,320]{1,0:T(8,128)S(1)} %collective-permute-done.11.z_ref, f32[32,320]{1,0:T(8,128)S(1)} %collective-permute-done.12.both_ref), custom_call_target="tpu_custom_call" | custom-call | tf_op jit(solution)/shard_map/pallas_call | solution.py:335
  (27 shorter events, 0.9 us)
Async XLA Ops:
  0.6 28.0 %copy-start.4 = (f32[1,64,2,32]{1,3,2,0:T(8,128)S(1)}, f32[1,64,2,32]{1,3,2,0:T(8,128)}, u32[]{:S(2)}) copy-start(f32[1,64,2,32]{1,3,2,0:T(8,128)} %param.6) | copy-start | bytes 49156
  0.7 0.9 copy-start.2
  1.6 27.1 %copy-start.3 = (bf16[1,78,8,128]{3,2,1,0:T(8,128)(2,1)S(1)}, bf16[1,78,8,128]{3,2,1,0:T(8,128)(2,1)}, u32[]{:S(2)}) copy-start(bf16[1,78,8,128]{3,2,1,0:T(8,128)(2,1)} %param.4) | copy-start | bytes 479236
  24.3 51.6 %all-to-all-start.1 = ((bf16[8,80,512]{2,1,0:T(8,128)(2,1)}), bf16[8,80,512]{2,1,0:T(8,128)(2,1)S(1)}, u32[]{:S(2)}, u32[]{:S(2)}) async-start(bf16[8,80,512]{2,1,0:T(8,128)(2,1)} %bitcast.4), calls=%async_computation.1 | async-start | bytes 1310720 | tf_op jit(solution)/shard_map/all_to_all | solution.py:283
  29.8 4.4 %collective-permute-start = (bf16[384,128]{1,0:T(8,128)(2,1)S(1)}, bf16[384,128]{1,0:T(8,128)(2,1)S(1)}, u32[]{:S(2)}, u32[]{:S(2)}) collective-permute-start(bf16[384,128]{1,0:T(8,128)(2,1)S(1)} %get-tuple-element.15), channel_id=1, source_target_pairs={{0,64},{64,0},{128,192},{192,128},{1,65},{65,1},{129,193},{193,129... | collective-permute-start | bytes 294920 | tf_op jit(solution)/shard_map/ppermute | solution.py:275
  32.5 5.2 %collective-permute-start.1 = (bf16[384,128]{1,0:T(8,128)(2,1)S(1)}, bf16[384,128]{1,0:T(8,128)(2,1)S(1)}, u32[]{:S(2)}, u32[]{:S(2)}) collective-permute-start(bf16[384,128]{1,0:T(8,128)(2,1)S(1)} %get-tuple-element.14), channel_id=1, source_target_pairs={{0,128},{64,192},{128,0},{192,64},{1,129},{65,193},{129,1},{193,65... | collective-permute-start | bytes 294920 | tf_op jit(solution)/shard_map/ppermute | solution.py:275
  34.2 5.6 %collective-permute-start.2 = (bf16[384,128]{1,0:T(8,128)(2,1)S(1)}, bf16[384,128]{1,0:T(8,128)(2,1)S(1)}, u32[]{:S(2)}, u32[]{:S(2)}) collective-permute-start(bf16[384,128]{1,0:T(8,128)(2,1)S(1)} %collective-permute-done), channel_id=1, source_target_pairs={{0,128},{64,192},{128,0},{192,64},{1,129},{65,193},{129,1},{193,65... | collective-permute-start | bytes 294920 | tf_op jit(solution)/shard_map/ppermute | solution.py:275
  39.9 19.5 %collective-permute-start.5 = (bf16[4,384,128]{2,1,0:T(8,128)(2,1)S(1)}, bf16[4,384,128]{2,1,0:T(8,128)(2,1)S(1)}, u32[]{:S(2)}, u32[]{:S(2)}) collective-permute-start(bf16[4,384,128]{2,1,0:T(8,128)(2,1)S(1)} %pad_maximum_fusion.refs_0_), channel_id=1, source_target_pairs={{0,3},{1,2},{2,1},{3,0},{4,7},{5,6},{6,5},{7,4},{8,11},{9,10},{10,... | collective-permute-start | bytes 1179656 | tf_op jit(solution)/shard_map/ppermute | solution.py:275
  42.5 16.8 %collective-permute-start.4 = (bf16[4,384,128]{2,1,0:T(8,128)(2,1)S(1)}, bf16[4,384,128]{2,1,0:T(8,128)(2,1)S(1)}, u32[]{:S(2)}, u32[]{:S(2)}) collective-permute-start(bf16[4,384,128]{2,1,0:T(8,128)(2,1)S(1)} %pad_maximum_fusion.refs_0_), channel_id=1, source_target_pairs={{0,2},{1,3},{2,0},{3,1},{4,6},{5,7},{6,4},{7,5},{8,10},{9,11},{10,... | collective-permute-start | bytes 1179656 | tf_op jit(solution)/shard_map/ppermute | solution.py:275
  43.1 16.3 %collective-permute-start.3 = (bf16[4,384,128]{2,1,0:T(8,128)(2,1)S(1)}, bf16[4,384,128]{2,1,0:T(8,128)(2,1)S(1)}, u32[]{:S(2)}, u32[]{:S(2)}) collective-permute-start(bf16[4,384,128]{2,1,0:T(8,128)(2,1)S(1)} %pad_maximum_fusion.refs_0_), channel_id=1, source_target_pairs={{0,1},{1,0},{2,3},{3,2},{4,5},{5,4},{6,7},{7,6},{8,9},{9,8},{10,11... | collective-permute-start | bytes 1179656 | tf_op jit(solution)/shard_map/ppermute | solution.py:275
  62.0 19.5 %copy-start.5 = (f32[64]{0:T(128)S(1)}, f32[64]{0:T(128)}, u32[]{:S(2)}) copy-start(f32[64]{0:T(128)} %param.7) | copy-start | bytes 772
  62.0 8.7 %collective-permute-start.6 = (bf16[768,128]{1,0:T(8,128)(2,1)S(1)}, bf16[768,128]{1,0:T(8,128)(2,1)S(1)}, u32[]{:S(2)}, u32[]{:S(2)}) collective-permute-start(bf16[768,128]{1,0:T(8,128)(2,1)S(1)} %get-tuple-element.17), channel_id=1, source_target_pairs={{0,60},{4,0},{8,4},{12,8},{16,12},{20,16},{24,20},{28,24},{32,28},... | collective-permute-start | bytes 589832 | tf_op jit(solution)/shard_map/ppermute | solution.py:291
  63.4 12.5 %collective-permute-start.7 = (bf16[768,128]{1,0:T(8,128)(2,1)S(1)}, bf16[768,128]{1,0:T(8,128)(2,1)S(1)}, u32[]{:S(2)}, u32[]{:S(2)}) collective-permute-start(bf16[768,128]{1,0:T(8,128)(2,1)S(1)} %get-tuple-element.18), channel_id=1, source_target_pairs={{0,4},{4,8},{8,12},{12,16},{16,20},{20,24},{24,28},{28,32},{32,36}... | collective-permute-start | bytes 589832 | tf_op jit(solution)/shard_map/ppermute | solution.py:292
  78.4 0.9 copy-start
  79.3 3.6 %collective-permute-start.8 = (f32[64,1280]{1,0:T(8,128)S(1)}, f32[64,1280]{1,0:T(8,128)}, u32[]{:S(2)}, u32[]{:S(2)}) collective-permute-start(f32[64,1280]{1,0:T(8,128)S(1)} %get-tuple-element.19.refs_0_), channel_id=1, source_target_pairs={{0,64},{64,0},{128,192},{192,128},{1,65},{65,1},{129,193},{193,129... | collective-permute-start | bytes 983048 | tf_op jit(solution)/shard_map/ppermute | solution.py:308
  82.9 1.1 copy-start.1
  87.6 1.7 %collective-permute-start.9 = (f32[64,1280]{1,0:T(8,128)S(1)}, f32[64,1280]{1,0:T(8,128)S(1)}, u32[]{:S(2)}, u32[]{:S(2)}) collective-permute-start(f32[64,1280]{1,0:T(8,128)S(1)} %get-tuple-element.22.refs_1_), channel_id=1, source_target_pairs={{0,64},{64,0},{128,192},{192,128},{1,65},{65,1},{129,193},{193,129... | collective-permute-start | bytes 983048 | tf_op jit(solution)/shard_map/ppermute | solution.py:319
  110.7 4.0 %collective-permute-start.12 = (f32[32,320]{1,0:T(8,128)S(1)}, f32[32,320]{1,0:T(8,128)S(1)}, u32[]{:S(2)}, u32[]{:S(2)}) collective-permute-start(f32[32,320]{1,0:T(8,128)S(1)} %shard_map.66.own_ref), channel_id=1, source_target_pairs={{0,192},{64,128},{128,64},{192,0},{1,193},{65,129},{129,65},{193,1... | collective-permute-start | bytes 122888 | tf_op jit(solution)/shard_map/ppermute | solution.py:334
  110.8 5.8 %collective-permute-start.11 = (f32[32,320]{1,0:T(8,128)S(1)}, f32[32,320]{1,0:T(8,128)S(1)}, u32[]{:S(2)}, u32[]{:S(2)}) collective-permute-start(f32[32,320]{1,0:T(8,128)S(1)} %shard_map.66.own_ref), channel_id=1, source_target_pairs={{0,128},{64,192},{128,0},{192,64},{1,129},{65,193},{129,1},{193,65... | collective-permute-start | bytes 122888 | tf_op jit(solution)/shard_map/ppermute | solution.py:334
  114.0 2.7 %collective-permute-start.10 = (f32[32,320]{1,0:T(8,128)S(1)}, f32[32,320]{1,0:T(8,128)S(1)}, u32[]{:S(2)}, u32[]{:S(2)}) collective-permute-start(f32[32,320]{1,0:T(8,128)S(1)} %shard_map.66.own_ref), channel_id=1, source_target_pairs={{0,64},{64,0},{128,192},{192,128},{1,65},{65,1},{129,193},{193,129... | collective-permute-start | bytes 122888 | tf_op jit(solution)/shard_map/ppermute | solution.py:334

commit v3 on v2

v3 whole, which is shorter than its diff:
```python
import math

import jax
import jax.numpy as jnp
from jax import lax
from jax.experimental import pallas as pl
from jax.experimental.pallas import tpu as pltpu
from jax.sharding import PartitionSpec as P


ITERS = 2
STEP_SIZE = 0.5
F32 = jnp.float32
BF16 = jnp.bfloat16
COMBOS = [(h, a, b) for h in (0, 1) for a in (0, 1) for b in (0, 1)]
MAIN = 1024
LANES = 1280
HALF = 320
PACK = 384
SIDE = 96


def iota(shape, dim):
    return lax.broadcasted_iota(jnp.int32, shape, dim)


def dot(a, b):
    return jnp.dot(a, b, preferred_element_type=F32)


def dot_t(a, b):
    return lax.dot_general(a, b, (((1,), (1,)), ((), ())), preferred_element_type=F32)


def onehot(test):
    return jnp.where(test, 1.0, 0.0).astype(BF16)


def two(x):
    high = x.astype(BF16)
    return high, (x - high.astype(F32)).astype(BF16)


def three(x):
    high = x.astype(BF16)
    rest = x - high.astype(F32)
    middle = rest.astype(BF16)
    return high, middle, (rest - middle.astype(F32)).astype(BF16)


def call(kernel, outs, scratch=(), smem=0, n_in=1, space=pltpu.VMEM):
    vmem = pl.BlockSpec(memory_space=pltpu.VMEM)
    held = pl.BlockSpec(memory_space=space)
    specs = [pl.BlockSpec(memory_space=pltpu.SMEM)] * smem + [held] * (n_in - smem)
    shapes = [jax.ShapeDtypeStruct(s, d) for s, d in outs]
    return pl.pallas_call(
        kernel,
        out_shape=shapes if len(shapes) > 1 else shapes[0],
        in_specs=specs,
        out_specs=[vmem] * len(shapes) if len(shapes) > 1 else vmem,
        scratch_shapes=list(scratch),
        compiler_params=pltpu.CompilerParams(vmem_limit_bytes=16 * 1024 * 1024),
    )


def edge_kernel(x_ref, z_ref, west_ref, east_ref):
    high, low = two(z_ref[...])
    codes = jnp.concatenate([high, low], axis=0)
    row, col = iota((128, 128), 0), iota((128, 128), 1)
    for first, out_ref in ((0, west_ref), (28, east_ref)):
        total = jnp.zeros((80, 128), F32)
        wanted = (first + (col & 3)) * 4 + ((col >> 3) & 3)
        for r in range(8):
            pick = (row == wanted) & ((col >> 5) == r % 4) & (((col >> 2) & 1) == r // 4)
            total = total + dot(x_ref[r], onehot(pick))
        out_ref[0:80, :] = total.astype(BF16)
        lane = iota((64, 128), 1)
        pick = (lane < 8) & (iota((64, 128), 0) == (lane >> 2) * 32 + first + (lane & 3))
        narrow = dot(codes, onehot(pick))
        edge = narrow[0:8]
        for group in range(1, 16):
            edge = edge + pltpu.roll(narrow[group * 8 : group * 8 + 8], group * 8, 1)
        out_ref[80:96, :] = jnp.concatenate([edge, jnp.zeros((8, 128), F32)], axis=0).astype(BF16)


def pack_kernel(place_ref, x_ref, z_ref, own_ref, other_ref):
    row, col = iota((128, 128), 0), iota((128, 128), 1)
    order = onehot(((row & 3) * 32 + (row >> 2)) == col)
    lane = iota((80, 128), 1)
    high, low = two(z_ref[...])
    codes = jnp.concatenate([high, low], axis=1)
    for flip, out_ref in enumerate((own_ref, other_ref)):
        first = (place_ref[0] ^ flip) * 2
        split = [dot(x_ref[p2 * 4 + first + u_lo], order) for u_lo in range(2) for p2 in range(2)]
        for v in range(4):
            piece = jnp.zeros((80, 128), F32)
            for slot in range(4):
                by = ((slot - v) % 4) * 32
                moved = pltpu.roll(split[slot], by, 1) if by else split[slot]
                piece = jnp.where((lane >> 5) == slot, moved, piece)
            out_ref[v * 80 : v * 80 + 80, :] = piece.astype(BF16)
        out_ref[HALF:PACK, :] = codes


def side_kernel(place_ref, east_ref, west_ref, own_ref, other_ref):
    row, col = iota((128, 128), 0), iota((128, 128), 1)
    is_east = (col & 7) < 4
    within = ((col >> 3) & 1) * 4 + (col & 3)
    sides = []
    for part in range(2):
        pick = row == (2 * (col >> 4) + part) * 8 + within
        east = dot(east_ref[80:96, :], onehot(pick & is_east))
        west = dot(west_ref[80:96, :], onehot(pick & jnp.logical_not(is_east)))
        sides.append((east + west)[0:8])
    codes = jnp.concatenate(sides, axis=0).astype(BF16)
    for flip, out_ref in enumerate((own_ref, other_ref)):
        pick = row == ((place_ref[0] ^ flip) * 8 + (col >> 4)) * 8 + within
        east = dot(east_ref[0:80, :], onehot(pick & is_east))
        west = dot(west_ref[0:80, :], onehot(pick & jnp.logical_not(is_east)))
        out_ref[0:80, :] = (east + west).astype(BF16)
        out_ref[80:SIDE, :] = codes


def unpack_kernel(place_ref, *refs):
    main_ref, edge_ref, left_ref, side_ref, hours, edges, arrived = refs[8:]
    copies = [
        pltpu.make_async_copy(refs[i], hours.at[i] if i < 4 else edges.at[i - 4], arrived.at[i]) for i in range(8)
    ]
    for copy in copies:
        copy.start()
    lane = iota((PACK, 128), 1)
    for pair in range(8):
        if pair % 2 == 0:
            copies[pair // 2].wait()
        even = hours[pair // 2, 2 * (pair % 2)].astype(F32)
        odd = hours[pair // 2, 2 * (pair % 2) + 1].astype(F32)
        lanes = slice(pair * 128, pair * 128 + 128)
        left_ref[0:PACK, lanes] = jnp.where(lane < 64, even, pltpu.roll(odd, 64, 1)).astype(BF16)
        left_ref[PACK : 2 * PACK, lanes] = jnp.where(lane < 64, pltpu.roll(even, 64, 1), odd).astype(BF16)
    lat, hour = 2 * place_ref[1] + place_ref[0], place_ref[2]
    for block in range(4):
        n = iota((1024, 256), 1) + block * 256
        slab = (((n >> 3) & 3) ^ hour) * 4 + (((n >> 1) & 3) ^ lat)
        source = slab * 64 + (n & 1) * 32 + (n >> 5)
        order = onehot(iota((1024, 256), 0) == source)
        main_ref[:, block * 256 : block * 256 + 256] = dot(left_ref[...], order).astype(BF16)
    lane = iota((SIDE, 128), 1)
    for copy in copies[4:]:
        copy.wait()
    for half in range(2):
        slabs = [edges[half * 2 + s // 4, s % 4].astype(F32) for s in range(8)]
        for group in range(8):
            piece = jnp.zeros((SIDE, 128), F32)
            for s in range(8):
                by = ((s - group) % 8) * 16
                moved = pltpu.roll(slabs[s], by, 1) if by else slabs[s]
                piece = jnp.where((lane >> 4) == s, moved, piece)
            side_ref[group * 96 : group * 96 + 96, half * 128 : half * 128 + 128] = piece.astype(BF16)
    n = iota((256, 256), 1)
    slab = (((n >> 3) & 3) ^ hour) * 4 + (((n >> 1) & 3) ^ lat)
    order = onehot(iota((256, 256), 0) == slab * 16 + (n & 1) * 8 + (n >> 5))
    sides = dot(side_ref[...], order).astype(BF16)
    for group in range(8):
        at = (group // 4) * PACK + (group % 4) * 80
        edge_ref[at : at + 80, :] = sides[group * 96 : group * 96 + 80]
        at = (group // 4) * PACK + HALF + (group % 4) * 16
        edge_ref[at : at + 16, :] = sides[group * 96 + 80 : group * 96 + 96]


def slice_kernel(place_ref, d_ref, out_ref, rows_ref):
    rows_ref[...] = jnp.zeros((512, 128), F32)
    for i in range(78):
        h, half = i // 39, i % 39
        part = d_ref[:, i * 128 : i * 128 + 128].astype(F32)
        for k in range(4):
            at = (k * 2 + h) * 64 + half
            rows_ref[at : at + 1, :] = part[k : k + 1, :]
    which = iota((32, 128), 0)
    want = ((which >> 2) & 1) * 64 + ((which >> 1) & 1) * 32 + place_ref[0] * 8 + (which & 1) * 4 + (which >> 3)
    picked = dot_t(onehot(iota((32, 128), 1) == want), rows_ref[...].astype(BF16))
    lane = iota((4, 128), 1)
    for v in range(4):
        for k in range(4):
            pair = picked[v * 8 : v * 8 + 8, k * 128 : k * 128 + 128]
            turned = pltpu.roll(pair, 64, 1)
            even = jnp.where(lane < 64, pair[0:4], turned[4:8])
            odd = jnp.where(lane < 64, turned[0:4], pair[4:8])
            for ab in range(4):
                at = v * 32 + ab * 4 + k
                rows_ref[at : at + 1, :] = even[ab : ab + 1, :]
                rows_ref[at + 16 : at + 17, :] = odd[ab : ab + 1, :]
    sent = rows_ref[0:128, :].astype(BF16)
    for peer in range(16):
        out_ref[peer] = sent


def turn_kernel(in_ref, out_ref, rows_ref):
    for v in range(4):
        for peer in range(16):
            part = in_ref[peer, v * 32 : v * 32 + 32].astype(F32)
            for hab in range(8):
                at = hab * 64 + peer * 4
                rows_ref[v, at : at + 4, :] = part[hab * 4 : hab * 4 + 4, :]
        turned = rows_ref[v].T
        kept = jnp.concatenate([turned[0:40], turned[64:104]], axis=0)
        out_ref[v * 80 : v * 80 + 80, :] = kept.astype(BF16)


def shifted_codes(codes, z_ref):
    lane = iota((1, LANES), 1)
    t, p = (lane >> 3) & 3, lane & 7
    for index, (h, a, b) in enumerate(COMBOS):
        by = 32 * b + 8 * h + a
        moved = pltpu.roll(codes, by, 1) if by else codes
        kept = jnp.where((t >= h) & (p >= a), moved, 0.0)
        z_ref[index * 64 : index * 64 + 64, :] = kept.astype(BF16)


def partial_adjoint(z, b_ref, bt_ref, x_ref, edge_ref, z_ref, r_ref, u_ref):
    for chunk in range(5):
        lanes = slice(chunk * 256, chunk * 256 + 256)
        codes = z_ref[:, lanes]
        for slot in range(2):
            rows = slice(slot * HALF, slot * HALF + HALF)
            held = pl.ds(pl.multiple_of((z ^ slot) * PACK, PACK), HALF)
            x = x_ref[held, lanes] if chunk < 4 else edge_ref[held, :]
            r_ref[rows, :] = (dot(b_ref[rows, :], codes) - x.astype(F32)).astype(BF16)
        u_ref[:, lanes] = dot(bt_ref[...], r_ref[...])
    lane = iota((1, LANES), 1)
    t, p = (lane >> 3) & 3, lane & 7
    total = u_ref[0:64, :]
    for index, (h, a, b) in enumerate(COMBOS[1:], 1):
        moved = pltpu.roll(u_ref[index * 64 : index * 64 + 64, :], LANES - (32 * b + 8 * h + a), 1)
        total = total + jnp.where((t < 4 - h) & (p < 8 - a), moved, 0.0)
    return total


def first_kernel(place_ref, own_ref, other_ref, x_ref, edge_ref, sum_ref, y_ref, b_ref, bt_ref, z_ref, r_ref, u_ref):
    b_ref[0:HALF, :] = own_ref[...]
    b_ref[HALF : 2 * HALF, :] = other_ref[...]
    bt_ref[...] = b_ref[...].T

    def rows_of(start, count):
        part = slice(start, start + count)
        return jnp.concatenate([x_ref[part, :], edge_ref[part, :]], axis=1).astype(F32)

    codes = rows_of(HALF, 64) + rows_of(PACK + HALF, 64)
    y_ref[...] = codes
    shifted_codes(codes, z_ref)
    sum_ref[...] = partial_adjoint(place_ref[1], b_ref, bt_ref, x_ref, edge_ref, z_ref, r_ref, u_ref)


def shrunk(moving, gradient, limits):
    same = iota((64, 64), 0) == iota((64, 64), 1)
    shrink = STEP_SIZE * jnp.sum(jnp.where(same, limits, 0.0), axis=1, keepdims=True)
    descent = moving - STEP_SIZE * gradient
    size = jnp.maximum(jnp.abs(descent) - shrink, 0.0)
    return jnp.where(descent < 0.0, -size, size)


def middle_kernel(factor, place_ref, mine_ref, other_ref, moving_ref, current_ref, limit_ref, bt_ref, b_ref, x_ref, edge_ref, sum_ref, y_ref, now_ref, z_ref, r_ref, u_ref):
    updated = shrunk(moving_ref[...], mine_ref[...] + other_ref[...], limit_ref[...])
    moving = updated + factor * (updated - current_ref[...])
    now_ref[...] = updated
    y_ref[...] = moving
    shifted_codes(moving, z_ref)
    sum_ref[...] = partial_adjoint(place_ref[1], b_ref, bt_ref, x_ref, edge_ref, z_ref, r_ref, u_ref)


def last_kernel(scale, place_ref, mine_ref, other_ref, moving_ref, limit_ref, b_ref, x_ref, codes_ref, grad_ref, z_ref, g_ref):
    codes = shrunk(moving_ref[...], mine_ref[...] + other_ref[...], limit_ref[...])
    core, z, t = place_ref[0], place_ref[1], place_ref[2]
    own = iota((MAIN, 128), 1)
    source = (own & 31) * 32 + t * 8 + (2 * z + core) * 2 + ((own >> 5) & 1)
    order = onehot((iota((MAIN, 128), 0) == source) & (own < 64))
    high, middle, low = three(codes[:, 0:MAIN])
    codes_ref[...] = (dot(high, order) + dot(middle, order)) + dot(low, order)
    shifted_codes(codes, z_ref)
    z_main = z_ref[:, 0:MAIN]
    x = x_ref[pl.ds(pl.multiple_of(z * PACK, 16), HALF), :]
    residual = (dot(b_ref[0:HALF, :], z_main) - x.astype(F32)).astype(BF16)
    g_ref[...] = dot_t(z_main, residual) * scale
    for peer in range(16):
        parts = [g_ref[hab * 64 + peer * 4 : hab * 64 + peer * 4 + 4, :] for hab in range(8)]
        grad_ref[peer] = jnp.concatenate(parts, axis=0).astype(BF16)


def add_kernel(in_ref, out_ref):
    total = in_ref[0].astype(F32)
    for peer in range(1, 16):
        total = total + in_ref[peer].astype(F32)
    out_ref[...] = total


def place_kernel(place_ref, own_ref, core_ref, z_ref, both_ref, out_ref, parts_ref, rows_ref):
    core, z = place_ref[0], place_ref[1]
    for flip, piece in enumerate((own_ref, core_ref, z_ref, both_ref)):
        u = 2 * (core ^ (flip & 1)) + (z ^ (flip >> 1))
        for v in range(4):
            low = v * 80 // 128 * 128
            turn = v * 80 - low
            lanes = piece[:, low : min(low + 256, HALF)]
            if lanes.shape[1] < 256:
                lanes = jnp.concatenate([lanes, jnp.zeros((32, 256 - lanes.shape[1]), F32)], axis=1)
            moved = pltpu.roll(lanes, 256 - turn, 1) if turn else lanes
            parts_ref[u * 4 + v] = moved[:, 0:128]
    for k in range(4):
        for h in range(2):
            for ab in range(4):
                row = (h * 4 + ab) * 4 + k
                for uv in range(16):
                    at = (ab // 2) * 32 + (uv // 4) * 8 + (ab % 2) * 4 + uv % 4
                    rows_ref[at : at + 1, :] = parts_ref[uv, row : row + 1, :]
            even = rows_ref[...]
            odd = pltpu.roll(even, 88, 1)
            turned = jnp.concatenate([even, odd], axis=0).T
            for i in range(39):
                lanes = slice((h * 39 + i) * 128, (h * 39 + i) * 128 + 128)
                out_ref[k : k + 1, lanes] = turned[i : i + 1, :]


def program(signal, dictionary, codes_init, thresholds):
    lat, tm = lax.axis_index("lat"), lax.axis_index("tm")
    z, core = lat // 2, lat % 2
    place = jnp.stack([core, z, tm]).astype(jnp.int32)
    lon = lax.axis_size("lon")

    ring = [[(i, (i + by) % lon) for i in range(lon)] for by in (-1, 1)]

    def flipped(block, axis, by):
        return lax.ppermute(block, axis, [(i, i ^ by) for i in range(4)])

    rows = signal[0].reshape(39, 2, 8, 128).transpose(2, 1, 0, 3)
    rows = jnp.pad(rows, ((0, 0), (0, 0), (0, 1), (0, 0))).reshape(8, 80, 128)
    start = codes_init[0].reshape(64, 64)

    def joined(kept, given):
        beside = flipped(given, "lat", 1)
        bands = [kept, beside, flipped(kept, "lat", 2), flipped(beside, "lat", 2)]
        hour = jnp.stack(bands)
        return [hour] + [flipped(hour, "tm", by) for by in (1, 2, 3)]

    west, east = call(edge_kernel, [((SIDE, 128), BF16)] * 2, n_in=2)(rows, start)
    east, west = lax.ppermute(west, "lon", ring[0]), lax.ppermute(east, "lon", ring[1])
    packed = call(pack_kernel, [((PACK, 128), BF16)] * 2, (), 1, 3)(place, rows, start)
    fields = joined(*packed)
    sides = call(side_kernel, [((SIDE, 128), BF16)] * 2, (), 1, 3)(place, east, west)
    sides = joined(*sides)
    sliced = call(slice_kernel, [((16, 128, 128), BF16)], [pltpu.VMEM((512, 128), F32)], 1, 2)(
        (2 * core + z).astype(jnp.int32).reshape(1), dictionary
    )
    sliced = lax.all_to_all(sliced, "lon", 0, 0, tiled=True)
    turned = call(turn_kernel, [((HALF, 512), BF16)], [pltpu.VMEM((4, 512, 128), F32)])(sliced)
    turned_other = flipped(turned, "lat", 2)
    x, edge = call(
        unpack_kernel,
        [((2 * PACK, MAIN), BF16), ((2 * PACK, 256), BF16)],
        [
            pltpu.VMEM((2 * PACK, MAIN), BF16),
            pltpu.VMEM((2 * PACK, 256), BF16),
            pltpu.VMEM((4, 4, PACK, 128), BF16),
            pltpu.VMEM((4, 4, SIDE, 128), BF16),
            pltpu.SemaphoreType.DMA((8,)),
        ],
        1,
        9,
        pltpu.HBM,
    )(place, *fields, *sides)

    work = [
        pltpu.VMEM((512, LANES), BF16),
        pltpu.VMEM((640, 256), BF16),
        pltpu.VMEM((512, LANES), F32),
    ]
    state = ((64, LANES), F32)
    limits = thresholds.reshape(1, 64)
    mine, moving, blocks, blocks_t = call(
        first_kernel, [state, state, ((640, 512), BF16), ((512, 640), BF16)], work, 1, 5
    )(place, turned, turned_other, x, edge)
    swap = [(i, i ^ 1) for i in range(4)]
    current = moving
    momentum_now = 1.0
    for _ in range(ITERS - 1):
        other = lax.ppermute(mine, "lat", swap)
        momentum_next = (1.0 + math.sqrt(1.0 + 4.0 * momentum_now * momentum_now)) / 2.0
        factor = (momentum_now - 1.0) / momentum_next
        momentum_now = momentum_next

        def step(*refs):
            middle_kernel(factor, *refs)

        mine, moving, current = call(step, [state, state, state], work, 1, 10)(
            place, mine, other, moving, current, limits, blocks_t, blocks, x, edge
        )
    other = lax.ppermute(mine, "lat", swap)
    positions = lax.axis_size("tm") * lax.axis_size("lat") * lon * 64

    def ending(*refs):
        last_kernel(1.0 / math.sqrt(positions), *refs)

    codes, grad = call(
        ending,
        [((64, 128), F32), ((16, 32, HALF), BF16)],
        [pltpu.VMEM((512, LANES), BF16), pltpu.VMEM((512, HALF), F32)],
        1,
        7,
    )(place, mine, other, moving, limits, blocks, x)
    grad = lax.all_to_all(grad, "lon", 0, 0, tiled=True)
    summed = call(add_kernel, [((32, HALF), F32)])(grad)
    others = [lax.ppermute(summed, "lat", [(i, i ^ flip) for i in range(4)]) for flip in (1, 2, 3)]
    gradient = call(
        place_kernel, [((4, 9984), F32)], [pltpu.VMEM((16, 32, 128), F32), pltpu.VMEM((64, 128), F32)], 1, 5
    )(place, summed, *others)
    return codes[:, :64].reshape(1, 64, 2, 32), gradient


def solution(mesh):
    placed = (P("tm", None, "lat", "lon"), P("lon", None), P("tm", None, "lat", "lon"), P())
    return jax.shard_map(
        program,
        mesh=mesh,
        in_specs=placed,
        out_specs=(P("tm", None, "lat", "lon"), P("lon", None)),
        check_vma=False,
    )
```

time: 120 us -> 117 us (0.975); the launches traced: 118 us -> 117 us
  blocking collectives: 40.2 us -> 16.1 us
  starting transfers between devices: 20.6 us -> 40.8 us
  Pallas kernels: 15.4 us -> 19.3 us
  local copies, waits for them, and re-layouts: 3.77 us -> 1.73 us
    all_to_all x1 -> x0, blocking collectives: 20.8 us -> none  [program(): sliced = lax.all_to_all(sliced, 'lon', 0, 0, tiled=True)]
    all_to_all x1, starting transfers between devices: 4.39 us -> 11.7 us  [program(): sliced = lax.all_to_all(sliced, 'lon', 0, 0, tiled=True)]
    ppermute x6 -> x13, starting transfers between devices: 8.67 us -> 14.3 us  [flipped(): return lax.ppermute(block, axis, [(i, i ^ by) for i in range(4)])]
    ppermute x2, starting transfers between devices: 1.54 us -> 5.95 us  [the longest x1 5.95 us: program(): lax.ppermute(west, 'lon', ring[0])]
    pallas_call x6 -> x8, Pallas kernels: 11.6 us -> 15.4 us  [the longest x1 5.33 us: program(): call(unpack_kernel, [((2 * PACK, MAIN), BF16), ((2 * PACK, 256), BF16)],...]
    all_to_all x1, blocking collectives: 19.4 us -> 16.1 us  [program(): grad = lax.all_to_all(grad, 'lon', 0, 0, tiled=True)]
    unnamed x12 -> x8, local copies, waits for them, and re-layouts: 2.84 us -> 0.89 us
    ppermute x2, starting transfers between devices: 2.68 us -> 4.38 us  [program(): other = lax.ppermute(mine, 'lat', swap)]
  transfers between devices with their start and end apart: 14 -> 21, of which waited for: 8 -> 10; matrix products, arithmetic and copies ran while one was open for 1% -> 1% of each run, Pallas kernels for 3% -> 7%
where the time goes in v3:
time: 117 us
  starting transfers between devices  40.8 us (35%)
  waiting for transfers between devices  38.1 us (33%)
  Pallas kernels  19.3 us (16%)
  blocking collectives  16.1 us (14%)
  local copies, waits for them, and re-layouts  1.73 us (1%)
    ppermute x13, waiting for transfers between devices, flipped(): return lax.ppermute(block, axis, [(i, i ^ by) for i in range(4)])  22 us
    all_to_all x1, blocking collectives, program(): grad = lax.all_to_all(grad, 'lon', 0, 0, tiled=True)  16.1 us
    ppermute x13, starting transfers between devices, flipped(): return lax.ppermute(block, axis, [(i, i ^ by) for i in range(4)])  14.3 us
    all_to_all x1, starting transfers between devices, program(): sliced = lax.all_to_all(sliced, 'lon', 0, 0, tiled=True)  11.7 us
    ppermute x1, waiting for transfers between devices, program(): lax.ppermute(east, 'lon', ring[1])  10.6 us
    ppermute x1, starting transfers between devices, program(): lax.ppermute(west, 'lon', ring[0])  5.95 us
    pallas_call x1, Pallas kernels, program(): call(unpack_kernel, [((2 * PACK, MAIN), BF16), ((2 * PACK, 256), BF16)],...  5.33 us
    ppermute x3, starting transfers between devices, program(): lax.ppermute(summed, 'lat', [(i, i ^ flip) for i in range(4)])  4.41 us
  transfers between devices with their start and end apart: 21, of which 10 were waited for; matrix products, arithmetic and copies ran while one was open for 1% of the time, Pallas kernels for 7%

profile of v3, /device:TPU:1, one launch (start us, length us, event | category | flops | bytes accessed | tf_op | source)
XLA Modules:
  0.0 117.0 jit_solution(7440975761855491514)
XLA Ops:
  0.7 0.9 copy-done
  1.6 1.2 %shard_map.59 = bf16[16,128,128]{2,1,0:T(8,128)(2,1)} custom-call(s32[1]{0:T(128)} %bitcast.3.place_ref, bf16[4,9984]{1,0:T(4,128)(2,1)S(1)} %copy-done), custom_call_target="tpu_custom_call" | custom-call | tf_op jit(solution)/shard_map/pallas_call | solution.py:349
  2.8 11.7 %all-to-all-start = ((bf16[16,128,128]{2,1,0:T(8,128)(2,1)}), bf16[16,128,128]{2,1,0:T(8,128)(2,1)S(1)}, u32[]{:S(2)}, u32[]{:S(2)}) async-start(bf16[16,128,128]{2,1,0:T(8,128)(2,1)} %shard_map.59), calls=%async_computation | async-start | bytes 1048576 | tf_op jit(solution)/shard_map/all_to_all | solution.py:352
  14.7 0.9 shard_map.61
  15.7 1.0 collective-permute-start.1
  16.7 0.7 collective-permute-start.2
  17.6 0.7 collective-permute-start.3
  18.9 5.9 %collective-permute-start.7 = (bf16[96,128]{1,0:T(8,128)(2,1)S(1)}, bf16[96,128]{1,0:T(8,128)(2,1)S(1)}, u32[]{:S(2)}, u32[]{:S(2)}) collective-permute-start(bf16[96,128]{1,0:T(8,128)(2,1)S(1)} %get-tuple-element.20), channel_id=1, source_target_pairs={{0,60},{4,0},{8,4},{12,8},{16,12},{20,16},{24,20},{28,24},{32,28},... | collective-permute-start | bytes 73736 | tf_op jit(solution)/shard_map/ppermute | solution.py:344
  24.8 1.0 collective-permute-done.7.east_ref
  25.8 10.6 %collective-permute-done.8.west_ref = bf16[96,128]{1,0:T(8,128)(2,1)S(1)} collective-permute-done((bf16[96,128]{1,0:T(8,128)(2,1)S(1)}, bf16[96,128]{1,0:T(8,128)(2,1)S(1)}, u32[]{:S(2)}, u32[]{:S(2)}) %collective-permute-start.8) | collective-permute-done | bytes 24608 | tf_op jit(solution)/shard_map/ppermute | solution.py:344
  36.4 0.8 shard_map.63
  37.2 2.1 %collective-permute-start.9 = (bf16[96,128]{1,0:T(8,128)(2,1)S(1)}, bf16[96,128]{1,0:T(8,128)(2,1)S(1)}, u32[]{:S(2)}, u32[]{:S(2)}) collective-permute-start(bf16[96,128]{1,0:T(8,128)(2,1)S(1)} %get-tuple-element.23), channel_id=1, source_target_pairs={{0,64},{64,0},{128,192},{192,128},{1,65},{65,1},{129,193},{193,129... | collective-permute-start | bytes 73736 | tf_op jit(solution)/shard_map/ppermute | solution.py:331
  39.3 0.8 collective-permute-done.9
  40.9 2.6 %collective-permute-start.6 = (bf16[4,384,128]{2,1,0:T(8,128)(2,1)S(1)}, bf16[4,384,128]{2,1,0:T(8,128)(2,1)S(1)}, u32[]{:S(2)}, u32[]{:S(2)}) collective-permute-start(bf16[4,384,128]{2,1,0:T(8,128)(2,1)S(1)} %pad_maximum_fusion.refs_0_), channel_id=1, source_target_pairs={{0,3},{1,2},{2,1},{3,0},{4,7},{5,6},{6,5},{7,4},{8,11},{9,10},{10,... | collective-permute-start | bytes 1179656 | tf_op jit(solution)/shard_map/ppermute | solution.py:331
  44.5 0.9 collective-permute-start
  45.5 2.6 %collective-permute-start.14 = (bf16[4,96,128]{2,1,0:T(8,128)(2,1)S(1)}, bf16[4,96,128]{2,1,0:T(8,128)(2,1)S(1)}, u32[]{:S(2)}, u32[]{:S(2)}) collective-permute-start(bf16[4,96,128]{2,1,0:T(8,128)(2,1)S(1)} %pad_maximum_fusion.1.refs_4_), channel_id=1, source_target_pairs={{0,3},{1,2},{2,1},{3,0},{4,7},{5,6},{6,5},{7,4},{8,11},{9,10},{10,... | collective-permute-start | bytes 294920 | tf_op jit(solution)/shard_map/ppermute | solution.py:331
  48.0 14.7 %collective-permute-done.14.refs_7_ = bf16[4,96,128]{2,1,0:T(8,128)(2,1)S(1)} collective-permute-done((bf16[4,96,128]{2,1,0:T(8,128)(2,1)S(1)}, bf16[4,96,128]{2,1,0:T(8,128)(2,1)S(1)}, u32[]{:S(2)}, u32[]{:S(2)}) %collective-permute-start.14) | collective-permute-done | bytes 98336 | tf_op jit(solution)/shard_map/ppermute | solution.py:331
  62.7 1.5 %collective-permute-start.13 = (bf16[4,96,128]{2,1,0:T(8,128)(2,1)S(1)}, bf16[4,96,128]{2,1,0:T(8,128)(2,1)S(1)}, u32[]{:S(2)}, u32[]{:S(2)}) collective-permute-start(bf16[4,96,128]{2,1,0:T(8,128)(2,1)S(1)} %pad_maximum_fusion.1.refs_4_), channel_id=1, source_target_pairs={{0,2},{1,3},{2,0},{3,1},{4,6},{5,7},{6,4},{7,5},{8,10},{9,11},{10,... | collective-permute-start | bytes 294920 | tf_op jit(solution)/shard_map/ppermute | solution.py:331
  64.3 3.4 %collective-permute-done.13.refs_6_ = bf16[4,96,128]{2,1,0:T(8,128)(2,1)S(1)} collective-permute-done((bf16[4,96,128]{2,1,0:T(8,128)(2,1)S(1)}, bf16[4,96,128]{2,1,0:T(8,128)(2,1)S(1)}, u32[]{:S(2)}, u32[]{:S(2)}) %collective-permute-start.13) | collective-permute-done | bytes 98336 | tf_op jit(solution)/shard_map/ppermute | solution.py:331
  68.3 2.8 %collective-permute-done.12.refs_5_ = bf16[4,96,128]{2,1,0:T(8,128)(2,1)S(1)} collective-permute-done((bf16[4,96,128]{2,1,0:T(8,128)(2,1)S(1)}, bf16[4,96,128]{2,1,0:T(8,128)(2,1)S(1)}, u32[]{:S(2)}, u32[]{:S(2)}) %collective-permute-start.12) | collective-permute-done | bytes 98336 | tf_op jit(solution)/shard_map/ppermute | solution.py:331
  71.2 5.3 %shard_map.64 = (bf16[768,1024]{1,0:T(8,128)(2,1)S(1)}, bf16[768,256]{1,0:T(8,128)(2,1)S(1)}) custom-call(s32[3]{0:T(128)S(1)} %pad_add_fusion.place_ref.refs_0_, bf16[4,384,128]{2,1,0:T(8,128)(2,1)S(1)} %pad_maximum_fusion.refs_0_, bf16[4,384,128]{2,1,0:T(8,128)(2,1)S(1)} %collective-permute-done.4.refs_1_, ...), custom_call_target="tpu_custom_call" | custom-call | tf_op jit(solution)/shard_map/pallas_call | solution.py:355
  76.5 3.2 %shard_map.65 = (f32[64,1280]{1,0:T(8,128)S(1)}, f32[64,1280]{1,0:T(8,128)S(1)}, bf16[640,512]{1,0:T(8,128)(2,1)S(1)}, bf16[512,640]{1,0:T(8,128)(2,1)S(1)}) custom-call(s32[3]{0:T(128)S(1)} %pad_add_fusion.place_ref.refs_0_, bf16[320,512]{1,0:T(8,128)(2,1)S(1)} %shard_map.60.own_ref, bf16[320,512]{1,0:T(8,128)(2,1)S(1)} %collective-permute-done.other_ref, ...), custom_call_target="tpu_custom_call" | custom-call | tf_op jit(solution)/shard_map/pallas_call | solution.py:377
  79.7 3.9 %collective-permute-start.15 = (f32[64,1280]{1,0:T(8,128)S(1)}, f32[64,1280]{1,0:T(8,128)S(1)}, u32[]{:S(2)}, u32[]{:S(2)}) collective-permute-start(f32[64,1280]{1,0:T(8,128)S(1)} %get-tuple-element.26.refs_1_), channel_id=1, source_target_pairs={{0,64},{64,0},{128,192},{192,128},{1,65},{65,1},{129,193},{193,129... | collective-permute-start | bytes 983048 | tf_op jit(solution)/shard_map/ppermute | solution.py:384
  83.6 1.3 %collective-permute-done.15.refs_2_ = f32[64,1280]{1,0:T(8,128)S(1)} collective-permute-done((f32[64,1280]{1,0:T(8,128)S(1)}, f32[64,1280]{1,0:T(8,128)S(1)}, u32[]{:S(2)}, u32[]{:S(2)}) %collective-permute-start.15) | collective-permute-done | bytes 327712 | tf_op jit(solution)/shard_map/ppermute | solution.py:384
  84.9 3.3 %shard_map.66 = (f32[64,1280]{1,0:T(8,128)S(1)}, f32[64,1280]{1,0:T(8,128)S(1)}, f32[64,1280]{1,0:T(8,128)}) custom-call(s32[3]{0:T(128)S(1)} %pad_add_fusion.place_ref.refs_0_, f32[64,1280]{1,0:T(8,128)S(1)} %get-tuple-element.26.refs_1_, f32[64,1280]{1,0:T(8,128)S(1)} %collective-permute-done.15.refs_2_, f32[64,1280]{1,0:T(8,128)S(1)} %get-tuple-element.27.refs_3_.refs_4_, ...), custom_call_target="tpu_custom_call" | custom-call | tf_op jit(solution)/shard_map/pallas_call | solution.py:392
  88.6 1.3 %collective-permute-done.16.refs_2_ = f32[64,1280]{1,0:T(8,128)S(1)} collective-permute-done((f32[64,1280]{1,0:T(8,128)S(1)}, f32[64,1280]{1,0:T(8,128)S(1)}, u32[]{:S(2)}, u32[]{:S(2)}) %collective-permute-start.16) | collective-permute-done | bytes 327712 | tf_op jit(solution)/shard_map/ppermute | solution.py:395
  89.9 2.0 %shard_map.67 = (f32[64,128]{1,0:T(8,128)S(1)}, bf16[16,32,320]{2,1,0:T(8,128)(2,1)S(1)}) custom-call(s32[3]{0:T(128)S(1)} %pad_add_fusion.place_ref.refs_0_, f32[64,1280]{1,0:T(8,128)S(1)} %get-tuple-element.30.refs_1_, f32[64,1280]{1,0:T(8,128)S(1)} %collective-permute-done.16.refs_2_, f32[64,1280]{1,0:T(8,128)S(1)} %get-tuple-element.31.refs_3_, ...), custom_call_target="tpu_custom_call" | custom-call | tf_op jit(solution)/shard_map/pallas_call | solution.py:401
  91.9 16.1 %all_to_all.10.in_ref = bf16[16,32,320]{2,1,0:T(8,128)(2,1)S(1)} all-to-all(bf16[16,32,320]{2,1,0:T(8,128)(2,1)S(1)} %get-tuple-element.33), channel_id=1, replica_groups=mesh['lat'=4,'lon'=16,'tm'=4] {'lon'}, dimensions={0} | all-to-all | bytes 655360 | tf_op jit(solution)/shard_map/all_to_all | solution.py:408
  108.1 2.6 %collective-permute-start.19 = (f32[32,320]{1,0:T(8,128)S(1)}, f32[32,320]{1,0:T(8,128)S(1)}, u32[]{:S(2)}, u32[]{:S(2)}) collective-permute-start(f32[32,320]{1,0:T(8,128)S(1)} %shard_map.68.own_ref), channel_id=1, source_target_pairs={{0,192},{64,128},{128,64},{192,0},{1,193},{65,129},{129,65},{193,1... | collective-permute-start | bytes 122888 | tf_op jit(solution)/shard_map/ppermute | solution.py:410
  110.7 1.8 %collective-permute-start.18 = (f32[32,320]{1,0:T(8,128)S(1)}, f32[32,320]{1,0:T(8,128)S(1)}, u32[]{:S(2)}, u32[]{:S(2)}) collective-permute-start(f32[32,320]{1,0:T(8,128)S(1)} %shard_map.68.own_ref), channel_id=1, source_target_pairs={{0,128},{64,192},{128,0},{192,64},{1,129},{65,193},{129,1},{193,65... | collective-permute-start | bytes 122888 | tf_op jit(solution)/shard_map/ppermute | solution.py:410
  113.2 2.0 %collective-permute-done.18.z_ref = f32[32,320]{1,0:T(8,128)S(1)} collective-permute-done((f32[32,320]{1,0:T(8,128)S(1)}, f32[32,320]{1,0:T(8,128)S(1)}, u32[]{:S(2)}, u32[]{:S(2)}) %collective-permute-start.18) | collective-permute-done | bytes 40992 | tf_op jit(solution)/shard_map/ppermute | solution.py:410
  115.1 1.8 %shard_map.69 = f32[4,9984]{1,0:T(4,128)} custom-call(s32[3]{0:T(128)S(1)} %pad_add_fusion.place_ref.refs_0_, f32[32,320]{1,0:T(8,128)S(1)} %shard_map.68.own_ref, f32[32,320]{1,0:T(8,128)S(1)} %collective-permute-done.17.core_ref, f32[32,320]{1,0:T(8,128)S(1)} %collective-permute-done.18.z_ref, f32[32,320]{1,0:T(8,128)S(1)} %collective-permute-done.19.both_ref), custom_call_target="tpu_custom_call" | custom-call | tf_op jit(solution)/shard_map/pallas_call | solution.py:411
  (37 shorter events, 4.5 us)
Async XLA Ops:
  0.6 13.9 %copy-start.3 = (f32[1,64,2,32]{1,3,2,0:T(8,128)S(1)}, f32[1,64,2,32]{1,3,2,0:T(8,128)}, u32[]{:S(2)}) copy-start(f32[1,64,2,32]{1,3,2,0:T(8,128)} %param.6) | copy-start | bytes 49156
  0.7 0.9 copy-start
  1.6 13.0 %copy-start.2 = (bf16[1,78,8,128]{3,2,1,0:T(8,128)(2,1)S(1)}, bf16[1,78,8,128]{3,2,1,0:T(8,128)(2,1)}, u32[]{:S(2)}) copy-start(bf16[1,78,8,128]{3,2,1,0:T(8,128)(2,1)} %param.4) | copy-start | bytes 479236
  2.8 41.5 %all-to-all-start = ((bf16[16,128,128]{2,1,0:T(8,128)(2,1)}), bf16[16,128,128]{2,1,0:T(8,128)(2,1)S(1)}, u32[]{:S(2)}, u32[]{:S(2)}) async-start(bf16[16,128,128]{2,1,0:T(8,128)(2,1)} %shard_map.59), calls=%async_computation | async-start | bytes 1048576 | tf_op jit(solution)/shard_map/all_to_all | solution.py:352
  15.7 2.0 %collective-permute-start.1 = (bf16[384,128]{1,0:T(8,128)(2,1)S(1)}, bf16[384,128]{1,0:T(8,128)(2,1)S(1)}, u32[]{:S(2)}, u32[]{:S(2)}) collective-permute-start(bf16[384,128]{1,0:T(8,128)(2,1)S(1)} %get-tuple-element.19), channel_id=1, source_target_pairs={{0,64},{64,0},{128,192},{192,128},{1,65},{65,1},{129,193},{193,129... | collective-permute-start | bytes 294920 | tf_op jit(solution)/shard_map/ppermute | solution.py:331
  16.7 24.1 %collective-permute-start.2 = (bf16[384,128]{1,0:T(8,128)(2,1)S(1)}, bf16[384,128]{1,0:T(8,128)(2,1)S(1)}, u32[]{:S(2)}, u32[]{:S(2)}) collective-permute-start(bf16[384,128]{1,0:T(8,128)(2,1)S(1)} %get-tuple-element.18), channel_id=1, source_target_pairs={{0,128},{64,192},{128,0},{192,64},{1,129},{65,193},{129,1},{193,65... | collective-permute-start | bytes 294920 | tf_op jit(solution)/shard_map/ppermute | solution.py:331
  17.6 23.2 %collective-permute-start.3 = (bf16[384,128]{1,0:T(8,128)(2,1)S(1)}, bf16[384,128]{1,0:T(8,128)(2,1)S(1)}, u32[]{:S(2)}, u32[]{:S(2)}) collective-permute-start(bf16[384,128]{1,0:T(8,128)(2,1)S(1)} %collective-permute-done.1), channel_id=1, source_target_pairs={{0,128},{64,192},{128,0},{192,64},{1,129},{65,193},{129,1},{193,65... | collective-permute-start | bytes 294920 | tf_op jit(solution)/shard_map/ppermute | solution.py:331
  18.9 6.9 %collective-permute-start.7 = (bf16[96,128]{1,0:T(8,128)(2,1)S(1)}, bf16[96,128]{1,0:T(8,128)(2,1)S(1)}, u32[]{:S(2)}, u32[]{:S(2)}) collective-permute-start(bf16[96,128]{1,0:T(8,128)(2,1)S(1)} %get-tuple-element.20), channel_id=1, source_target_pairs={{0,60},{4,0},{8,4},{12,8},{16,12},{20,16},{24,20},{28,24},{32,28},... | collective-permute-start | bytes 73736 | tf_op jit(solution)/shard_map/ppermute | solution.py:344
  24.8 11.6 %collective-permute-start.8 = (bf16[96,128]{1,0:T(8,128)(2,1)S(1)}, bf16[96,128]{1,0:T(8,128)(2,1)S(1)}, u32[]{:S(2)}, u32[]{:S(2)}) collective-permute-start(bf16[96,128]{1,0:T(8,128)(2,1)S(1)} %get-tuple-element.21), channel_id=1, source_target_pairs={{0,4},{4,8},{8,12},{12,16},{16,20},{20,24},{24,28},{28,32},{32,36}... | collective-permute-start | bytes 73736 | tf_op jit(solution)/shard_map/ppermute | solution.py:344
  37.2 3.0 %collective-permute-start.9 = (bf16[96,128]{1,0:T(8,128)(2,1)S(1)}, bf16[96,128]{1,0:T(8,128)(2,1)S(1)}, u32[]{:S(2)}, u32[]{:S(2)}) collective-permute-start(bf16[96,128]{1,0:T(8,128)(2,1)S(1)} %get-tuple-element.23), channel_id=1, source_target_pairs={{0,64},{64,0},{128,192},{192,128},{1,65},{65,1},{129,193},{193,129... | collective-permute-start | bytes 73736 | tf_op jit(solution)/shard_map/ppermute | solution.py:331
  39.3 5.2 %collective-permute-start.10 = (bf16[96,128]{1,0:T(8,128)(2,1)S(1)}, bf16[96,128]{1,0:T(8,128)(2,1)S(1)}, u32[]{:S(2)}, u32[]{:S(2)}) collective-permute-start(bf16[96,128]{1,0:T(8,128)(2,1)S(1)} %get-tuple-element.22), channel_id=1, source_target_pairs={{0,128},{64,192},{128,0},{192,64},{1,129},{65,193},{129,1},{193,65... | collective-permute-start | bytes 73736 | tf_op jit(solution)/shard_map/ppermute | solution.py:331
  40.2 5.3 %collective-permute-start.11 = (bf16[96,128]{1,0:T(8,128)(2,1)S(1)}, bf16[96,128]{1,0:T(8,128)(2,1)S(1)}, u32[]{:S(2)}, u32[]{:S(2)}) collective-permute-start(bf16[96,128]{1,0:T(8,128)(2,1)S(1)} %collective-permute-done.9), channel_id=1, source_target_pairs={{0,128},{64,192},{128,0},{192,64},{1,129},{65,193},{129,1},{193,65... | collective-permute-start | bytes 73736 | tf_op jit(solution)/shard_map/ppermute | solution.py:331
  40.9 30.3 %collective-permute-start.6 = (bf16[4,384,128]{2,1,0:T(8,128)(2,1)S(1)}, bf16[4,384,128]{2,1,0:T(8,128)(2,1)S(1)}, u32[]{:S(2)}, u32[]{:S(2)}) collective-permute-start(bf16[4,384,128]{2,1,0:T(8,128)(2,1)S(1)} %pad_maximum_fusion.refs_0_), channel_id=1, source_target_pairs={{0,3},{1,2},{2,1},{3,0},{4,7},{5,6},{6,5},{7,4},{8,11},{9,10},{10,... | collective-permute-start | bytes 1179656 | tf_op jit(solution)/shard_map/ppermute | solution.py:331
  43.4 27.7 %collective-permute-start.5 = (bf16[4,384,128]{2,1,0:T(8,128)(2,1)S(1)}, bf16[4,384,128]{2,1,0:T(8,128)(2,1)S(1)}, u32[]{:S(2)}, u32[]{:S(2)}) collective-permute-start(bf16[4,384,128]{2,1,0:T(8,128)(2,1)S(1)} %pad_maximum_fusion.refs_0_), channel_id=1, source_target_pairs={{0,2},{1,3},{2,0},{3,1},{4,6},{5,7},{6,4},{7,5},{8,10},{9,11},{10,... | collective-permute-start | bytes 1179656 | tf_op jit(solution)/shard_map/ppermute | solution.py:331
  44.0 27.2 %collective-permute-start.4 = (bf16[4,384,128]{2,1,0:T(8,128)(2,1)S(1)}, bf16[4,384,128]{2,1,0:T(8,128)(2,1)S(1)}, u32[]{:S(2)}, u32[]{:S(2)}) collective-permute-start(bf16[4,384,128]{2,1,0:T(8,128)(2,1)S(1)} %pad_maximum_fusion.refs_0_), channel_id=1, source_target_pairs={{0,1},{1,0},{2,3},{3,2},{4,5},{5,4},{6,7},{7,6},{8,9},{9,8},{10,11... | collective-permute-start | bytes 1179656 | tf_op jit(solution)/shard_map/ppermute | solution.py:331
  44.5 32.0 %collective-permute-start = (bf16[320,512]{1,0:T(8,128)(2,1)S(1)}, bf16[320,512]{1,0:T(8,128)(2,1)S(1)}, u32[]{:S(2)}, u32[]{:S(2)}) collective-permute-start(bf16[320,512]{1,0:T(8,128)(2,1)S(1)} %shard_map.60.own_ref), channel_id=1, source_target_pairs={{0,128},{64,192},{128,0},{192,64},{1,129},{65,193},{129,1},{193,65... | collective-permute-start | bytes 983048 | tf_op jit(solution)/shard_map/ppermute | solution.py:331
  45.5 17.2 %collective-permute-start.14 = (bf16[4,96,128]{2,1,0:T(8,128)(2,1)S(1)}, bf16[4,96,128]{2,1,0:T(8,128)(2,1)S(1)}, u32[]{:S(2)}, u32[]{:S(2)}) collective-permute-start(bf16[4,96,128]{2,1,0:T(8,128)(2,1)S(1)} %pad_maximum_fusion.1.refs_4_), channel_id=1, source_target_pairs={{0,3},{1,2},{2,1},{3,0},{4,7},{5,6},{6,5},{7,4},{8,11},{9,10},{10,... | collective-permute-start | bytes 294920 | tf_op jit(solution)/shard_map/ppermute | solution.py:331
  62.7 5.0 %collective-permute-start.13 = (bf16[4,96,128]{2,1,0:T(8,128)(2,1)S(1)}, bf16[4,96,128]{2,1,0:T(8,128)(2,1)S(1)}, u32[]{:S(2)}, u32[]{:S(2)}) collective-permute-start(bf16[4,96,128]{2,1,0:T(8,128)(2,1)S(1)} %pad_maximum_fusion.1.refs_4_), channel_id=1, source_target_pairs={{0,2},{1,3},{2,0},{3,1},{4,6},{5,7},{6,4},{7,5},{8,10},{9,11},{10,... | collective-permute-start | bytes 294920 | tf_op jit(solution)/shard_map/ppermute | solution.py:331
  67.7 3.5 %collective-permute-start.12 = (bf16[4,96,128]{2,1,0:T(8,128)(2,1)S(1)}, bf16[4,96,128]{2,1,0:T(8,128)(2,1)S(1)}, u32[]{:S(2)}, u32[]{:S(2)}) collective-permute-start(bf16[4,96,128]{2,1,0:T(8,128)(2,1)S(1)} %pad_maximum_fusion.1.refs_4_), channel_id=1, source_target_pairs={{0,1},{1,0},{2,3},{3,2},{4,5},{5,4},{6,7},{7,6},{8,9},{9,8},{10,11... | collective-permute-start | bytes 294920 | tf_op jit(solution)/shard_map/ppermute | solution.py:331
  76.5 8.4 %copy-start.1 = (f32[64]{0:T(128)S(1)}, f32[64]{0:T(128)}, u32[]{:S(2)}) copy-start(f32[64]{0:T(128)} %param.7) | copy-start | bytes 772
  79.7 5.2 %collective-permute-start.15 = (f32[64,1280]{1,0:T(8,128)S(1)}, f32[64,1280]{1,0:T(8,128)S(1)}, u32[]{:S(2)}, u32[]{:S(2)}) collective-permute-start(f32[64,1280]{1,0:T(8,128)S(1)} %get-tuple-element.26.refs_1_), channel_id=1, source_target_pairs={{0,64},{64,0},{128,192},{192,128},{1,65},{65,1},{129,193},{193,129... | collective-permute-start | bytes 983048 | tf_op jit(solution)/shard_map/ppermute | solution.py:384
  88.2 1.7 %collective-permute-start.16 = (f32[64,1280]{1,0:T(8,128)S(1)}, f32[64,1280]{1,0:T(8,128)S(1)}, u32[]{:S(2)}, u32[]{:S(2)}) collective-permute-start(f32[64,1280]{1,0:T(8,128)S(1)} %get-tuple-element.30.refs_1_), channel_id=1, source_target_pairs={{0,64},{64,0},{128,192},{192,128},{1,65},{65,1},{129,193},{193,129... | collective-permute-start | bytes 983048 | tf_op jit(solution)/shard_map/ppermute | solution.py:395
  108.1 5.1 %collective-permute-start.19 = (f32[32,320]{1,0:T(8,128)S(1)}, f32[32,320]{1,0:T(8,128)S(1)}, u32[]{:S(2)}, u32[]{:S(2)}) collective-permute-start(f32[32,320]{1,0:T(8,128)S(1)} %shard_map.68.own_ref), channel_id=1, source_target_pairs={{0,192},{64,128},{128,64},{192,0},{1,193},{65,129},{129,65},{193,1... | collective-permute-start | bytes 122888 | tf_op jit(solution)/shard_map/ppermute | solution.py:410
  110.7 4.5 %collective-permute-start.18 = (f32[32,320]{1,0:T(8,128)S(1)}, f32[32,320]{1,0:T(8,128)S(1)}, u32[]{:S(2)}, u32[]{:S(2)}) collective-permute-start(f32[32,320]{1,0:T(8,128)S(1)} %shard_map.68.own_ref), channel_id=1, source_target_pairs={{0,128},{64,192},{128,0},{192,64},{1,129},{65,193},{129,1},{193,65... | collective-permute-start | bytes 122888 | tf_op jit(solution)/shard_map/ppermute | solution.py:410
  112.5 2.7 %collective-permute-start.17 = (f32[32,320]{1,0:T(8,128)S(1)}, f32[32,320]{1,0:T(8,128)S(1)}, u32[]{:S(2)}, u32[]{:S(2)}) collective-permute-start(f32[32,320]{1,0:T(8,128)S(1)} %shard_map.68.own_ref), channel_id=1, source_target_pairs={{0,64},{64,0},{128,192},{192,128},{1,65},{65,1},{129,193},{193,129... | collective-permute-start | bytes 122888 | tf_op jit(solution)/shard_map/ppermute | solution.py:410

commit v4 on v3

--- a/solution.py
+++ b/solution.py
@@ -121,13 +121,17 @@
         out_ref[80:SIDE, :] = codes
 
 
-def unpack_kernel(place_ref, *refs):
-    main_ref, edge_ref, left_ref, side_ref, hours, edges, arrived = refs[8:]
-    copies = [
-        pltpu.make_async_copy(refs[i], hours.at[i] if i < 4 else edges.at[i - 4], arrived.at[i]) for i in range(8)
-    ]
+def fetched(refs, held, arrived):
+    copies = [pltpu.make_async_copy(ref, held.at[i], arrived.at[i]) for i, ref in enumerate(refs)]
     for copy in copies:
         copy.start()
+    return copies
+
+
+def unpack_kernel(place_ref, *refs):
+    main_ref, token_ref, left_ref, hours, arrived = refs[4:]
+    token_ref[...] = jnp.zeros((8, 128), F32)
+    copies = fetched(refs[:4], hours, arrived)
     lane = iota((PACK, 128), 1)
     for pair in range(8):
         if pair % 2 == 0:
@@ -144,8 +148,17 @@
         source = slab * 64 + (n & 1) * 32 + (n >> 5)
         order = onehot(iota((1024, 256), 0) == source)
         main_ref[:, block * 256 : block * 256 + 256] = dot(left_ref[...], order).astype(BF16)
+
+
+def unpack_side_kernel(place_ref, *refs):
+    edge_ref, side_ref, edges, arrived = refs[5:]
+    copies = fetched(refs[:4], edges, arrived)
+    lat, hour = 2 * place_ref[1] + place_ref[0], place_ref[2]
+    n = iota((256, 256), 1)
+    slab = (((n >> 3) & 3) ^ hour) * 4 + (((n >> 1) & 3) ^ lat)
+    order = onehot(iota((256, 256), 0) == slab * 16 + (n & 1) * 8 + (n >> 5))
     lane = iota((SIDE, 128), 1)
-    for copy in copies[4:]:
+    for copy in copies:
         copy.wait()
     for half in range(2):
         slabs = [edges[half * 2 + s // 4, s % 4].astype(F32) for s in range(8)]
@@ -156,15 +169,25 @@
                 moved = pltpu.roll(slabs[s], by, 1) if by else slabs[s]
                 piece = jnp.where((lane >> 4) == s, moved, piece)
             side_ref[group * 96 : group * 96 + 96, half * 128 : half * 128 + 128] = piece.astype(BF16)
-    n = iota((256, 256), 1)
-    slab = (((n >> 3) & 3) ^ hour) * 4 + (((n >> 1) & 3) ^ lat)
-    order = onehot(iota((256, 256), 0) == slab * 16 + (n & 1) * 8 + (n >> 5))
     sides = dot(side_ref[...], order).astype(BF16)
     for group in range(8):
         at = (group // 4) * PACK + (group % 4) * 80
         edge_ref[at : at + 80, :] = sides[group * 96 : group * 96 + 80]
         at = (group // 4) * PACK + HALF + (group % 4) * 16
         edge_ref[at : at + 16, :] = sides[group * 96 + 80 : group * 96 + 96]
+
+
+def dense(x):
+    last = x[:, 256:384]
+    lane = iota((16, 128), 1)
+    last = jnp.where(lane < 64, last[0:16], pltpu.roll(last[16:32], 64, 1))
+    return jnp.concatenate([x[:, 0:128], x[:, 128:256], last], axis=0)
+
+
+def spread(x):
+    last = x[64:80]
+    last = jnp.concatenate([last, pltpu.roll(last, 64, 1)], axis=0)
+    return jnp.concatenate([x[0:32], x[32:64], last], axis=1)
 
 
 def slice_kernel(place_ref, d_ref, out_ref, rows_ref):
@@ -189,21 +212,23 @@
                 at = v * 32 + ab * 4 + k
                 rows_ref[at : at + 1, :] = even[ab : ab + 1, :]
                 rows_ref[at + 16 : at + 17, :] = odd[ab : ab + 1, :]
-    sent = rows_ref[0:128, :].astype(BF16)
+    row, col = iota((128, 384), 0), iota((128, 384), 1)
+    total = jnp.zeros((32, 384), F32)
+    for v in range(4):
+        put = ((row & 63) < 40) & (col == v * 80 + (row >> 6) * 40 + (row & 63))
+        total = total + dot(rows_ref[v * 32 : v * 32 + 32, :].astype(BF16), onehot(put))
+    sent = dense(total).astype(BF16)
     for peer in range(16):
         out_ref[peer] = sent
 
 
 def turn_kernel(in_ref, out_ref, rows_ref):
-    for v in range(4):
-        for peer in range(16):
-            part = in_ref[peer, v * 32 : v * 32 + 32].astype(F32)
-            for hab in range(8):
-                at = hab * 64 + peer * 4
-                rows_ref[v, at : at + 4, :] = part[hab * 4 : hab * 4 + 4, :]
-        turned = rows_ref[v].T
-        kept = jnp.concatenate([turned[0:40], turned[64:104]], axis=0)
-        out_ref[v * 80 : v * 80 + 80, :] = kept.astype(BF16)
+    for peer in range(16):
+        part = spread(in_ref[peer].astype(F32))
+        for hab in range(8):
+            at = hab * 64 + peer * 4
+            rows_ref[at : at + 4, :] = part[hab * 4 : hab * 4 + 4, :]
+    out_ref[...] = rows_ref[...].T[0:HALF].astype(BF16)
 
 
 def shifted_codes(codes, z_ref):
@@ -279,10 +304,11 @@
     z_main = z_ref[:, 0:MAIN]
     x = x_ref[pl.ds(pl.multiple_of(z * PACK, 16), HALF), :]
     residual = (dot(b_ref[0:HALF, :], z_main) - x.astype(F32)).astype(BF16)
-    g_ref[...] = dot_t(z_main, residual) * scale
+    filled = jnp.concatenate([residual, jnp.zeros((64, MAIN), BF16)], axis=0)
+    g_ref[...] = dot_t(z_main, filled) * scale
     for peer in range(16):
         parts = [g_ref[hab * 64 + peer * 4 : hab * 64 + peer * 4 + 4, :] for hab in range(8)]
-        grad_ref[peer] = jnp.concatenate(parts, axis=0).astype(BF16)
+        grad_ref[peer] = dense(jnp.concatenate(parts, axis=0)).astype(BF16)
 
 
 def add_kernel(in_ref, out_ref):
@@ -296,13 +322,9 @@
     core, z = place_ref[0], place_ref[1]
     for flip, piece in enumerate((own_ref, core_ref, z_ref, both_ref)):
         u = 2 * (core ^ (flip & 1)) + (z ^ (flip >> 1))
+        whole = spread(piece[...])
         for v in range(4):
-            low = v * 80 // 128 * 128
-            turn = v * 80 - low
-            lanes = piece[:, low : min(low + 256, HALF)]
-            if lanes.shape[1] < 256:
-                lanes = jnp.concatenate([lanes, jnp.zeros((32, 256 - lanes.shape[1]), F32)], axis=1)
-            moved = pltpu.roll(lanes, 256 - turn, 1) if turn else lanes
+            moved = pltpu.roll(whole, 384 - v * 80, 1) if v else whole
             parts_ref[u * 4 + v] = moved[:, 0:128]
     for k in range(4):
         for h in range(2):
@@ -346,26 +368,36 @@
     fields = joined(*packed)
     sides = call(side_kernel, [((SIDE, 128), BF16)] * 2, (), 1, 3)(place, east, west)
     sides = joined(*sides)
-    sliced = call(slice_kernel, [((16, 128, 128), BF16)], [pltpu.VMEM((512, 128), F32)], 1, 2)(
+    sliced = call(slice_kernel, [((16, 80, 128), BF16)], [pltpu.VMEM((512, 128), F32)], 1, 2)(
         (2 * core + z).astype(jnp.int32).reshape(1), dictionary
     )
     sliced = lax.all_to_all(sliced, "lon", 0, 0, tiled=True)
-    turned = call(turn_kernel, [((HALF, 512), BF16)], [pltpu.VMEM((4, 512, 128), F32)])(sliced)
+    turned = call(turn_kernel, [((HALF, 512), BF16)], [pltpu.VMEM((512, 384), F32)])(sliced)
     turned_other = flipped(turned, "lat", 2)
-    x, edge = call(
+    x, token = call(
         unpack_kernel,
-        [((2 * PACK, MAIN), BF16), ((2 * PACK, 256), BF16)],
+        [((2 * PACK, MAIN), BF16), ((8, 128), F32)],
         [
             pltpu.VMEM((2 * PACK, MAIN), BF16),
-            pltpu.VMEM((2 * PACK, 256), BF16),
             pltpu.VMEM((4, 4, PACK, 128), BF16),
-            pltpu.VMEM((4, 4, SIDE, 128), BF16),
-            pltpu.SemaphoreType.DMA((8,)),
+            pltpu.SemaphoreType.DMA((4,)),
         ],
         1,
-        9,
+        5,
         pltpu.HBM,
-    )(place, *fields, *sides)
+    )(place, *fields)
+    edge = call(
+        unpack_side_kernel,
+        [((2 * PACK, 256), BF16)],
+        [
+            pltpu.VMEM((2 * PACK, 256), BF16),
+            pltpu.VMEM((4, 4, SIDE, 128), BF16),
+            pltpu.SemaphoreType.DMA((4,)),
+        ],
+        1,
+        6,
+        pltpu.HBM,
+    )(place, *sides, token)
 
     work = [
         pltpu.VMEM((512, LANES), BF16),
@@ -400,13 +432,13 @@
 
     codes, grad = call(
         ending,
-        [((64, 128), F32), ((16, 32, HALF), BF16)],
-        [pltpu.VMEM((512, LANES), BF16), pltpu.VMEM((512, HALF), F32)],
+        [((64, 128), F32), ((16, 80, 128), BF16)],
+        [pltpu.VMEM((512, LANES), BF16), pltpu.VMEM((512, 384), F32)],
         1,
         7,
     )(place, mine, other, moving, limits, blocks, x)
     grad = lax.all_to_all(grad, "lon", 0, 0, tiled=True)
-    summed = call(add_kernel, [((32, HALF), F32)])(grad)
+    summed = call(add_kernel, [((80, 128), F32)])(grad)
     others = [lax.ppermute(summed, "lat", [(i, i ^ flip) for i in range(4)]) for flip in (1, 2, 3)]
     gradient = call(
         place_kernel, [((4, 9984), F32)], [pltpu.VMEM((16, 32, 128), F32), pltpu.VMEM((64, 128), F32)], 1, 5

time: 117 us -> 106 us (0.906)
  waiting for transfers between devices: 38.1 us -> 22.3 us
  local copies, waits for them, and re-layouts: 1.73 us -> 3.4 us
  starting transfers between devices: 40.8 us -> 42.4 us
    ppermute x13, waiting for transfers between devices: 22 us -> 10.9 us  [flipped(): return lax.ppermute(block, axis, [(i, i ^ by) for i in range(4)])]
    ppermute x1, waiting for transfers between devices: 10.6 us -> 7.25 us  [program(): lax.ppermute(east, 'lon', ring[1])]
    ppermute x13, starting transfers between devices: 14.3 us -> 16.6 us  [flipped(): return lax.ppermute(block, axis, [(i, i ^ by) for i in range(4)])]
    pallas_call x5 -> x6, Pallas kernels: 8.85 us -> 9.44 us  [the longest x1 3.72 us: program(): call(unpack_kernel, [((2 * PACK, MAIN), BF16), ((8, 128), F32)], [pltpu.V...]
  transfers between devices with their start and end apart: 21 -> 21, of which waited for: 10 -> 11; matrix products, arithmetic and copies ran while one was open for 1% -> 3% of each run, Pallas kernels for 7% -> 8%
where the time goes in v4:
time: 106 us; the launch traced here: 105 us
  starting transfers between devices  42.4 us (40%)
  waiting for transfers between devices  22.3 us (21%)
  Pallas kernels  19.8 us (19%)
  blocking collectives  16.4 us (15%)
  local copies, waits for them, and re-layouts  3.4 us (3%)
    ppermute x13, starting transfers between devices, flipped(): return lax.ppermute(block, axis, [(i, i ^ by) for i in range(4)])  16.6 us
    all_to_all x1, blocking collectives, program(): grad = lax.all_to_all(grad, 'lon', 0, 0, tiled=True)  16.4 us
    all_to_all x1, starting transfers between devices, program(): sliced = lax.all_to_all(sliced, 'lon', 0, 0, tiled=True)  11.7 us
    ppermute x13, waiting for transfers between devices, flipped(): return lax.ppermute(block, axis, [(i, i ^ by) for i in range(4)])  10.9 us
    ppermute x1, waiting for transfers between devices, program(): lax.ppermute(east, 'lon', ring[1])  7.25 us
    ppermute x1, starting transfers between devices, program(): lax.ppermute(west, 'lon', ring[0])  5.76 us
    ppermute x2, starting transfers between devices, program(): other = lax.ppermute(mine, 'lat', swap)  4.55 us
    ppermute x3, starting transfers between devices, program(): lax.ppermute(summed, 'lat', [(i, i ^ flip) for i in range(4)])  3.77 us
  transfers between devices with their start and end apart: 21, of which 11 were waited for; matrix products, arithmetic and copies ran while one was open for 3% of the time, Pallas kernels for 8%

profile of v4, /device:TPU:1, one launch (start us, length us, event | category | flops | bytes accessed | tf_op | source)
XLA Modules:
  0.0 105.2 jit_solution(12665513783840989037)
XLA Ops:
  0.7 0.9 copy-done
  1.5 1.3 %shard_map.59 = bf16[16,80,128]{2,1,0:T(8,128)(2,1)} custom-call(s32[1]{0:T(128)} %bitcast.3.place_ref, bf16[4,9984]{1,0:T(4,128)(2,1)S(1)} %copy-done), custom_call_target="tpu_custom_call" | custom-call | tf_op jit(solution)/shard_map/pallas_call | solution.py:371
  2.8 11.7 %all-to-all-start = ((bf16[16,80,128]{2,1,0:T(8,128)(2,1)}), bf16[16,80,128]{2,1,0:T(8,128)(2,1)S(1)}, u32[]{:S(2)}, u32[]{:S(2)}) async-start(bf16[16,80,128]{2,1,0:T(8,128)(2,1)} %shard_map.59), calls=%async_computation | async-start | bytes 655360 | tf_op jit(solution)/shard_map/all_to_all | solution.py:374
  15.4 1.0 copy.14
  16.5 0.9 shard_map.61
  17.4 1.0 collective-permute-start.1
  20.1 4.8 %collective-permute-done.2 = bf16[384,128]{1,0:T(8,128)(2,1)S(1)} collective-permute-done((bf16[384,128]{1,0:T(8,128)(2,1)S(1)}, bf16[384,128]{1,0:T(8,128)(2,1)S(1)}, u32[]{:S(2)}, u32[]{:S(2)}) %collective-permute-start.2) | collective-permute-done | bytes 98336 | tf_op jit(solution)/shard_map/ppermute | solution.py:353
  24.9 2.1 %collective-permute-done.3 = bf16[384,128]{1,0:T(8,128)(2,1)S(1)} collective-permute-done((bf16[384,128]{1,0:T(8,128)(2,1)S(1)}, bf16[384,128]{1,0:T(8,128)(2,1)S(1)}, u32[]{:S(2)}, u32[]{:S(2)}) %collective-permute-start.3) | collective-permute-done | bytes 98336 | tf_op jit(solution)/shard_map/ppermute | solution.py:353
  27.1 2.6 %collective-permute-start.6 = (bf16[4,384,128]{2,1,0:T(8,128)(2,1)S(1)}, bf16[4,384,128]{2,1,0:T(8,128)(2,1)S(1)}, u32[]{:S(2)}, u32[]{:S(2)}) collective-permute-start(bf16[4,384,128]{2,1,0:T(8,128)(2,1)S(1)} %pad_maximum_fusion.refs_0_), channel_id=1, source_target_pairs={{0,3},{1,2},{2,1},{3,0},{4,7},{5,6},{6,5},{7,4},{8,11},{9,10},{10,... | collective-permute-start | bytes 1179656 | tf_op jit(solution)/shard_map/ppermute | solution.py:353
  30.9 5.8 %collective-permute-start.7 = (bf16[96,128]{1,0:T(8,128)(2,1)S(1)}, bf16[96,128]{1,0:T(8,128)(2,1)S(1)}, u32[]{:S(2)}, u32[]{:S(2)}) collective-permute-start(bf16[96,128]{1,0:T(8,128)(2,1)S(1)} %get-tuple-element.21), channel_id=1, source_target_pairs={{0,60},{4,0},{8,4},{12,8},{16,12},{20,16},{24,20},{28,24},{32,28},... | collective-permute-start | bytes 73736 | tf_op jit(solution)/shard_map/ppermute | solution.py:366
  36.9 1.0 collective-permute-start
  37.9 7.3 %collective-permute-done.8.west_ref = bf16[96,128]{1,0:T(8,128)(2,1)S(1)} collective-permute-done((bf16[96,128]{1,0:T(8,128)(2,1)S(1)}, bf16[96,128]{1,0:T(8,128)(2,1)S(1)}, u32[]{:S(2)}, u32[]{:S(2)}) %collective-permute-start.8) | collective-permute-done | bytes 24608 | tf_op jit(solution)/shard_map/ppermute | solution.py:366
  45.9 3.5 %collective-permute-start.9 = (bf16[96,128]{1,0:T(8,128)(2,1)S(1)}, bf16[96,128]{1,0:T(8,128)(2,1)S(1)}, u32[]{:S(2)}, u32[]{:S(2)}) collective-permute-start(bf16[96,128]{1,0:T(8,128)(2,1)S(1)} %get-tuple-element.24), channel_id=1, source_target_pairs={{0,64},{64,0},{128,192},{192,128},{1,65},{65,1},{129,193},{193,129... | collective-permute-start | bytes 73736 | tf_op jit(solution)/shard_map/ppermute | solution.py:353
  49.4 0.8 collective-permute-done.9
  50.3 1.4 %collective-permute-start.10 = (bf16[96,128]{1,0:T(8,128)(2,1)S(1)}, bf16[96,128]{1,0:T(8,128)(2,1)S(1)}, u32[]{:S(2)}, u32[]{:S(2)}) collective-permute-start(bf16[96,128]{1,0:T(8,128)(2,1)S(1)} %get-tuple-element.23), channel_id=1, source_target_pairs={{0,128},{64,192},{128,0},{192,64},{1,129},{65,193},{129,1},{193,65... | collective-permute-start | bytes 73736 | tf_op jit(solution)/shard_map/ppermute | solution.py:353
  51.7 1.2 %collective-permute-done.10 = bf16[96,128]{1,0:T(8,128)(2,1)S(1)} collective-permute-done((bf16[96,128]{1,0:T(8,128)(2,1)S(1)}, bf16[96,128]{1,0:T(8,128)(2,1)S(1)}, u32[]{:S(2)}, u32[]{:S(2)}) %collective-permute-start.10) | collective-permute-done | bytes 24608 | tf_op jit(solution)/shard_map/ppermute | solution.py:353
  52.9 1.4 %collective-permute-start.11 = (bf16[96,128]{1,0:T(8,128)(2,1)S(1)}, bf16[96,128]{1,0:T(8,128)(2,1)S(1)}, u32[]{:S(2)}, u32[]{:S(2)}) collective-permute-start(bf16[96,128]{1,0:T(8,128)(2,1)S(1)} %collective-permute-done.9), channel_id=1, source_target_pairs={{0,128},{64,192},{128,0},{192,64},{1,129},{65,193},{129,1},{193,65... | collective-permute-start | bytes 73736 | tf_op jit(solution)/shard_map/ppermute | solution.py:353
  54.4 1.2 %collective-permute-done.11 = bf16[96,128]{1,0:T(8,128)(2,1)S(1)} collective-permute-done((bf16[96,128]{1,0:T(8,128)(2,1)S(1)}, bf16[96,128]{1,0:T(8,128)(2,1)S(1)}, u32[]{:S(2)}, u32[]{:S(2)}) %collective-permute-start.11) | collective-permute-done | bytes 24608 | tf_op jit(solution)/shard_map/ppermute | solution.py:353
  55.6 2.6 %collective-permute-start.14 = (bf16[4,96,128]{2,1,0:T(8,128)(2,1)S(1)}, bf16[4,96,128]{2,1,0:T(8,128)(2,1)S(1)}, u32[]{:S(2)}, u32[]{:S(2)}) collective-permute-start(bf16[4,96,128]{2,1,0:T(8,128)(2,1)S(1)} %pad_maximum_fusion.1.refs_0_), channel_id=1, source_target_pairs={{0,3},{1,2},{2,1},{3,0},{4,7},{5,6},{6,5},{7,4},{8,11},{9,10},{10,... | collective-permute-start | bytes 294920 | tf_op jit(solution)/shard_map/ppermute | solution.py:353
  59.0 3.7 %shard_map.62 = (bf16[768,1024]{1,0:T(8,128)(2,1)S(1)}, f32[8,128]{1,0:T(8,128)S(1)}) custom-call(s32[3]{0:T(128)S(1)} %pad_add_fusion.place_ref.refs_0_, bf16[4,384,128]{2,1,0:T(8,128)(2,1)S(1)} %pad_maximum_fusion.refs_0_, bf16[4,384,128]{2,1,0:T(8,128)(2,1)S(1)} %collective-permute-done.4.refs_1_, ...), custom_call_target="tpu_custom_call" | custom-call | tf_op jit(solution)/shard_map/pallas_call | solution.py:377
  63.3 2.2 %shard_map.65.edge_ref.refs_9_ = bf16[768,256]{1,0:T(8,128)(2,1)S(1)} custom-call(s32[3]{0:T(128)S(1)} %pad_add_fusion.place_ref.refs_0_, bf16[4,96,128]{2,1,0:T(8,128)(2,1)S(1)} %pad_maximum_fusion.1.refs_0_, bf16[4,96,128]{2,1,0:T(8,128)(2,1)S(1)} %collective-permute-done.12.refs_1_, bf16[4,96,128]{2,1,0:T(8,128)(2,1)S(1)} %collective-permute-done.13.refs_2_, ...), custom_call_target="tpu_custom_call" | custom-call | tf_op jit(solution)/shard_map/pallas_call | solution.py:389
  65.5 3.1 %shard_map.66 = (f32[64,1280]{1,0:T(8,128)S(1)}, f32[64,1280]{1,0:T(8,128)S(1)}, bf16[640,512]{1,0:T(8,128)(2,1)S(1)}, bf16[512,640]{1,0:T(8,128)(2,1)S(1)}) custom-call(s32[3]{0:T(128)S(1)} %pad_add_fusion.place_ref.refs_0_, bf16[320,512]{1,0:T(8,128)(2,1)S(1)} %shard_map.60.own_ref, bf16[320,512]{1,0:T(8,128)(2,1)S(1)} %collective-permute-done.other_ref, ...), custom_call_target="tpu_custom_call" | custom-call | tf_op jit(solution)/shard_map/pallas_call | solution.py:409
  68.6 4.1 %collective-permute-start.15 = (f32[64,1280]{1,0:T(8,128)S(1)}, f32[64,1280]{1,0:T(8,128)S(1)}, u32[]{:S(2)}, u32[]{:S(2)}) collective-permute-start(f32[64,1280]{1,0:T(8,128)S(1)} %get-tuple-element.26.refs_1_), channel_id=1, source_target_pairs={{0,64},{64,0},{128,192},{192,128},{1,65},{65,1},{129,193},{193,129... | collective-permute-start | bytes 983048 | tf_op jit(solution)/shard_map/ppermute | solution.py:416
  72.7 1.3 %collective-permute-done.15.refs_2_ = f32[64,1280]{1,0:T(8,128)S(1)} collective-permute-done((f32[64,1280]{1,0:T(8,128)S(1)}, f32[64,1280]{1,0:T(8,128)S(1)}, u32[]{:S(2)}, u32[]{:S(2)}) %collective-permute-start.15) | collective-permute-done | bytes 327712 | tf_op jit(solution)/shard_map/ppermute | solution.py:416
  73.9 3.2 %shard_map.67 = (f32[64,1280]{1,0:T(8,128)S(1)}, f32[64,1280]{1,0:T(8,128)S(1)}, f32[64,1280]{1,0:T(8,128)}) custom-call(s32[3]{0:T(128)S(1)} %pad_add_fusion.place_ref.refs_0_, f32[64,1280]{1,0:T(8,128)S(1)} %get-tuple-element.26.refs_1_, f32[64,1280]{1,0:T(8,128)S(1)} %collective-permute-done.15.refs_2_, f32[64,1280]{1,0:T(8,128)S(1)} %get-tuple-element.27.refs_3_.refs_4_, ...), custom_call_target="tpu_custom_call" | custom-call | tf_op jit(solution)/shard_map/pallas_call | solution.py:424
  77.6 1.3 %collective-permute-done.16.refs_2_ = f32[64,1280]{1,0:T(8,128)S(1)} collective-permute-done((f32[64,1280]{1,0:T(8,128)S(1)}, f32[64,1280]{1,0:T(8,128)S(1)}, u32[]{:S(2)}, u32[]{:S(2)}) %collective-permute-start.16) | collective-permute-done | bytes 327712 | tf_op jit(solution)/shard_map/ppermute | solution.py:427
  78.8 2.0 %shard_map.68 = (f32[64,128]{1,0:T(8,128)S(1)}, bf16[16,80,128]{2,1,0:T(8,128)(2,1)S(1)}) custom-call(s32[3]{0:T(128)S(1)} %pad_add_fusion.place_ref.refs_0_, f32[64,1280]{1,0:T(8,128)S(1)} %get-tuple-element.30.refs_1_, f32[64,1280]{1,0:T(8,128)S(1)} %collective-permute-done.16.refs_2_, f32[64,1280]{1,0:T(8,128)S(1)} %get-tuple-element.31.refs_3_, ...), custom_call_target="tpu_custom_call" | custom-call | tf_op jit(solution)/shard_map/pallas_call | solution.py:433
  80.8 16.4 %all_to_all.10.in_ref = bf16[16,80,128]{2,1,0:T(8,128)(2,1)S(1)} all-to-all(bf16[16,80,128]{2,1,0:T(8,128)(2,1)S(1)} %get-tuple-element.33), channel_id=1, replica_groups=mesh['lat'=4,'lon'=16,'tm'=4] {'lon'}, dimensions={0} | all-to-all | bytes 655360 | tf_op jit(solution)/shard_map/all_to_all | solution.py:440
  97.2 1.8 %collective-permute-start.19 = (f32[80,128]{1,0:T(8,128)S(1)}, f32[80,128]{1,0:T(8,128)S(1)}, u32[]{:S(2)}, u32[]{:S(2)}) collective-permute-start(f32[80,128]{1,0:T(8,128)S(1)} %shard_map.69.own_ref), channel_id=1, source_target_pairs={{0,192},{64,128},{128,64},{192,0},{1,193},{65,129},{129,65},{193,1... | collective-permute-start | bytes 122888 | tf_op jit(solution)/shard_map/ppermute | solution.py:442
  99.1 1.9 %collective-permute-start.18 = (f32[80,128]{1,0:T(8,128)S(1)}, f32[80,128]{1,0:T(8,128)S(1)}, u32[]{:S(2)}, u32[]{:S(2)}) collective-permute-start(f32[80,128]{1,0:T(8,128)S(1)} %shard_map.69.own_ref), channel_id=1, source_target_pairs={{0,128},{64,192},{128,0},{192,64},{1,129},{65,193},{129,1},{193,65... | collective-permute-start | bytes 122888 | tf_op jit(solution)/shard_map/ppermute | solution.py:442
  101.7 1.6 %collective-permute-done.18.z_ref = f32[80,128]{1,0:T(8,128)S(1)} collective-permute-done((f32[80,128]{1,0:T(8,128)S(1)}, f32[80,128]{1,0:T(8,128)S(1)}, u32[]{:S(2)}, u32[]{:S(2)}) %collective-permute-start.18) | collective-permute-done | bytes 40992 | tf_op jit(solution)/shard_map/ppermute | solution.py:442
  103.3 1.9 %shard_map.70 = f32[4,9984]{1,0:T(4,128)} custom-call(s32[3]{0:T(128)S(1)} %pad_add_fusion.place_ref.refs_0_, f32[80,128]{1,0:T(8,128)S(1)} %shard_map.69.own_ref, f32[80,128]{1,0:T(8,128)S(1)} %collective-permute-done.17.core_ref, f32[80,128]{1,0:T(8,128)S(1)} %collective-permute-done.18.z_ref, f32[80,128]{1,0:T(8,128)S(1)} %collective-permute-done.19.both_ref), custom_call_target="tpu_custom_call" | custom-call | tf_op jit(solution)/shard_map/pallas_call | solution.py:443
  (34 shorter events, 7.5 us)
Async XLA Ops:
  0.7 0.9 copy-start
  2.8 33.8 %all-to-all-start = ((bf16[16,80,128]{2,1,0:T(8,128)(2,1)}), bf16[16,80,128]{2,1,0:T(8,128)(2,1)S(1)}, u32[]{:S(2)}, u32[]{:S(2)}) async-start(bf16[16,80,128]{2,1,0:T(8,128)(2,1)} %shard_map.59), calls=%async_computation | async-start | bytes 655360 | tf_op jit(solution)/shard_map/all_to_all | solution.py:374
  17.4 2.0 %collective-permute-start.1 = (bf16[384,128]{1,0:T(8,128)(2,1)S(1)}, bf16[384,128]{1,0:T(8,128)(2,1)S(1)}, u32[]{:S(2)}, u32[]{:S(2)}) collective-permute-start(bf16[384,128]{1,0:T(8,128)(2,1)S(1)} %get-tuple-element.19), channel_id=1, source_target_pairs={{0,64},{64,0},{128,192},{192,128},{1,65},{65,1},{129,193},{193,129... | collective-permute-start | bytes 294920 | tf_op jit(solution)/shard_map/ppermute | solution.py:353
  18.4 6.5 %collective-permute-start.2 = (bf16[384,128]{1,0:T(8,128)(2,1)S(1)}, bf16[384,128]{1,0:T(8,128)(2,1)S(1)}, u32[]{:S(2)}, u32[]{:S(2)}) collective-permute-start(bf16[384,128]{1,0:T(8,128)(2,1)S(1)} %get-tuple-element.18), channel_id=1, source_target_pairs={{0,128},{64,192},{128,0},{192,64},{1,129},{65,193},{129,1},{193,65... | collective-permute-start | bytes 294920 | tf_op jit(solution)/shard_map/ppermute | solution.py:353
  19.4 7.6 %collective-permute-start.3 = (bf16[384,128]{1,0:T(8,128)(2,1)S(1)}, bf16[384,128]{1,0:T(8,128)(2,1)S(1)}, u32[]{:S(2)}, u32[]{:S(2)}) collective-permute-start(bf16[384,128]{1,0:T(8,128)(2,1)S(1)} %collective-permute-done.1), channel_id=1, source_target_pairs={{0,128},{64,192},{128,0},{192,64},{1,129},{65,193},{129,1},{193,65... | collective-permute-start | bytes 294920 | tf_op jit(solution)/shard_map/ppermute | solution.py:353
  27.1 31.2 %collective-permute-start.6 = (bf16[4,384,128]{2,1,0:T(8,128)(2,1)S(1)}, bf16[4,384,128]{2,1,0:T(8,128)(2,1)S(1)}, u32[]{:S(2)}, u32[]{:S(2)}) collective-permute-start(bf16[4,384,128]{2,1,0:T(8,128)(2,1)S(1)} %pad_maximum_fusion.refs_0_), channel_id=1, source_target_pairs={{0,3},{1,2},{2,1},{3,0},{4,7},{5,6},{6,5},{7,4},{8,11},{9,10},{10,... | collective-permute-start | bytes 1179656 | tf_op jit(solution)/shard_map/ppermute | solution.py:353
  29.6 29.1 %collective-permute-start.5 = (bf16[4,384,128]{2,1,0:T(8,128)(2,1)S(1)}, bf16[4,384,128]{2,1,0:T(8,128)(2,1)S(1)}, u32[]{:S(2)}, u32[]{:S(2)}) collective-permute-start(bf16[4,384,128]{2,1,0:T(8,128)(2,1)S(1)} %pad_maximum_fusion.refs_0_), channel_id=1, source_target_pairs={{0,2},{1,3},{2,0},{3,1},{4,6},{5,7},{6,4},{7,5},{8,10},{9,11},{10,... | collective-permute-start | bytes 1179656 | tf_op jit(solution)/shard_map/ppermute | solution.py:353
  30.1 28.9 %collective-permute-start.4 = (bf16[4,384,128]{2,1,0:T(8,128)(2,1)S(1)}, bf16[4,384,128]{2,1,0:T(8,128)(2,1)S(1)}, u32[]{:S(2)}, u32[]{:S(2)}) collective-permute-start(bf16[4,384,128]{2,1,0:T(8,128)(2,1)S(1)} %pad_maximum_fusion.refs_0_), channel_id=1, source_target_pairs={{0,1},{1,0},{2,3},{3,2},{4,5},{5,4},{6,7},{7,6},{8,9},{9,8},{10,11... | collective-permute-start | bytes 1179656 | tf_op jit(solution)/shard_map/ppermute | solution.py:353
  30.9 7.0 %collective-permute-start.7 = (bf16[96,128]{1,0:T(8,128)(2,1)S(1)}, bf16[96,128]{1,0:T(8,128)(2,1)S(1)}, u32[]{:S(2)}, u32[]{:S(2)}) collective-permute-start(bf16[96,128]{1,0:T(8,128)(2,1)S(1)} %get-tuple-element.21), channel_id=1, source_target_pairs={{0,60},{4,0},{8,4},{12,8},{16,12},{20,16},{24,20},{28,24},{32,28},... | collective-permute-start | bytes 73736 | tf_op jit(solution)/shard_map/ppermute | solution.py:366
  36.9 28.6 %collective-permute-start = (bf16[320,512]{1,0:T(8,128)(2,1)S(1)}, bf16[320,512]{1,0:T(8,128)(2,1)S(1)}, u32[]{:S(2)}, u32[]{:S(2)}) collective-permute-start(bf16[320,512]{1,0:T(8,128)(2,1)S(1)} %shard_map.60.own_ref), channel_id=1, source_target_pairs={{0,128},{64,192},{128,0},{192,64},{1,129},{65,193},{129,1},{193,65... | collective-permute-start | bytes 983048 | tf_op jit(solution)/shard_map/ppermute | solution.py:353
  37.9 7.3 %collective-permute-start.8 = (bf16[96,128]{1,0:T(8,128)(2,1)S(1)}, bf16[96,128]{1,0:T(8,128)(2,1)S(1)}, u32[]{:S(2)}, u32[]{:S(2)}) collective-permute-start(bf16[96,128]{1,0:T(8,128)(2,1)S(1)} %get-tuple-element.22), channel_id=1, source_target_pairs={{0,4},{4,8},{8,12},{12,16},{16,20},{20,24},{24,28},{28,32},{32,36}... | collective-permute-start | bytes 73736 | tf_op jit(solution)/shard_map/ppermute | solution.py:366
  45.9 4.4 %collective-permute-start.9 = (bf16[96,128]{1,0:T(8,128)(2,1)S(1)}, bf16[96,128]{1,0:T(8,128)(2,1)S(1)}, u32[]{:S(2)}, u32[]{:S(2)}) collective-permute-start(bf16[96,128]{1,0:T(8,128)(2,1)S(1)} %get-tuple-element.24), channel_id=1, source_target_pairs={{0,64},{64,0},{128,192},{192,128},{1,65},{65,1},{129,193},{193,129... | collective-permute-start | bytes 73736 | tf_op jit(solution)/shard_map/ppermute | solution.py:353
  50.3 2.7 %collective-permute-start.10 = (bf16[96,128]{1,0:T(8,128)(2,1)S(1)}, bf16[96,128]{1,0:T(8,128)(2,1)S(1)}, u32[]{:S(2)}, u32[]{:S(2)}) collective-permute-start(bf16[96,128]{1,0:T(8,128)(2,1)S(1)} %get-tuple-element.23), channel_id=1, source_target_pairs={{0,128},{64,192},{128,0},{192,64},{1,129},{65,193},{129,1},{193,65... | collective-permute-start | bytes 73736 | tf_op jit(solution)/shard_map/ppermute | solution.py:353
  52.9 2.7 %collective-permute-start.11 = (bf16[96,128]{1,0:T(8,128)(2,1)S(1)}, bf16[96,128]{1,0:T(8,128)(2,1)S(1)}, u32[]{:S(2)}, u32[]{:S(2)}) collective-permute-start(bf16[96,128]{1,0:T(8,128)(2,1)S(1)} %collective-permute-done.9), channel_id=1, source_target_pairs={{0,128},{64,192},{128,0},{192,64},{1,129},{65,193},{129,1},{193,65... | collective-permute-start | bytes 73736 | tf_op jit(solution)/shard_map/ppermute | solution.py:353
  55.6 7.1 %collective-permute-start.14 = (bf16[4,96,128]{2,1,0:T(8,128)(2,1)S(1)}, bf16[4,96,128]{2,1,0:T(8,128)(2,1)S(1)}, u32[]{:S(2)}, u32[]{:S(2)}) collective-permute-start(bf16[4,96,128]{2,1,0:T(8,128)(2,1)S(1)} %pad_maximum_fusion.1.refs_0_), channel_id=1, source_target_pairs={{0,3},{1,2},{2,1},{3,0},{4,7},{5,6},{6,5},{7,4},{8,11},{9,10},{10,... | collective-permute-start | bytes 294920 | tf_op jit(solution)/shard_map/ppermute | solution.py:353
  58.2 5.0 %collective-permute-start.13 = (bf16[4,96,128]{2,1,0:T(8,128)(2,1)S(1)}, bf16[4,96,128]{2,1,0:T(8,128)(2,1)S(1)}, u32[]{:S(2)}, u32[]{:S(2)}) collective-permute-start(bf16[4,96,128]{2,1,0:T(8,128)(2,1)S(1)} %pad_maximum_fusion.1.refs_0_), channel_id=1, source_target_pairs={{0,2},{1,3},{2,0},{3,1},{4,6},{5,7},{6,4},{7,5},{8,10},{9,11},{10,... | collective-permute-start | bytes 294920 | tf_op jit(solution)/shard_map/ppermute | solution.py:353
  58.7 4.5 %collective-permute-start.12 = (bf16[4,96,128]{2,1,0:T(8,128)(2,1)S(1)}, bf16[4,96,128]{2,1,0:T(8,128)(2,1)S(1)}, u32[]{:S(2)}, u32[]{:S(2)}) collective-permute-start(bf16[4,96,128]{2,1,0:T(8,128)(2,1)S(1)} %pad_maximum_fusion.1.refs_0_), channel_id=1, source_target_pairs={{0,1},{1,0},{2,3},{3,2},{4,5},{5,4},{6,7},{7,6},{8,9},{9,8},{10,11... | collective-permute-start | bytes 294920 | tf_op jit(solution)/shard_map/ppermute | solution.py:353
  63.3 10.6 %copy-start.1 = (f32[64]{0:T(128)S(1)}, f32[64]{0:T(128)}, u32[]{:S(2)}) copy-start(f32[64]{0:T(128)} %param.7) | copy-start | bytes 772
  68.6 5.3 %collective-permute-start.15 = (f32[64,1280]{1,0:T(8,128)S(1)}, f32[64,1280]{1,0:T(8,128)S(1)}, u32[]{:S(2)}, u32[]{:S(2)}) collective-permute-start(f32[64,1280]{1,0:T(8,128)S(1)} %get-tuple-element.26.refs_1_), channel_id=1, source_target_pairs={{0,64},{64,0},{128,192},{192,128},{1,65},{65,1},{129,193},{193,129... | collective-permute-start | bytes 983048 | tf_op jit(solution)/shard_map/ppermute | solution.py:416
  77.1 1.7 %collective-permute-start.16 = (f32[64,1280]{1,0:T(8,128)S(1)}, f32[64,1280]{1,0:T(8,128)S(1)}, u32[]{:S(2)}, u32[]{:S(2)}) collective-permute-start(f32[64,1280]{1,0:T(8,128)S(1)} %get-tuple-element.30.refs_1_), channel_id=1, source_target_pairs={{0,64},{64,0},{128,192},{192,128},{1,65},{65,1},{129,193},{193,129... | collective-permute-start | bytes 983048 | tf_op jit(solution)/shard_map/ppermute | solution.py:427
  97.2 4.5 %collective-permute-start.19 = (f32[80,128]{1,0:T(8,128)S(1)}, f32[80,128]{1,0:T(8,128)S(1)}, u32[]{:S(2)}, u32[]{:S(2)}) collective-permute-start(f32[80,128]{1,0:T(8,128)S(1)} %shard_map.69.own_ref), channel_id=1, source_target_pairs={{0,192},{64,128},{128,64},{192,0},{1,193},{65,129},{129,65},{193,1... | collective-permute-start | bytes 122888 | tf_op jit(solution)/shard_map/ppermute | solution.py:442
  99.1 4.3 %collective-permute-start.18 = (f32[80,128]{1,0:T(8,128)S(1)}, f32[80,128]{1,0:T(8,128)S(1)}, u32[]{:S(2)}, u32[]{:S(2)}) collective-permute-start(f32[80,128]{1,0:T(8,128)S(1)} %shard_map.69.own_ref), channel_id=1, source_target_pairs={{0,128},{64,192},{128,0},{192,64},{1,129},{65,193},{129,1},{193,65... | collective-permute-start | bytes 122888 | tf_op jit(solution)/shard_map/ppermute | solution.py:442
  101.0 2.3 %collective-permute-start.17 = (f32[80,128]{1,0:T(8,128)S(1)}, f32[80,128]{1,0:T(8,128)S(1)}, u32[]{:S(2)}, u32[]{:S(2)}) collective-permute-start(f32[80,128]{1,0:T(8,128)S(1)} %shard_map.69.own_ref), channel_id=1, source_target_pairs={{0,64},{64,0},{128,192},{192,128},{1,65},{65,1},{129,193},{193,129... | collective-permute-start | bytes 122888 | tf_op jit(solution)/shard_map/ppermute | solution.py:442
